TPU v7x, 32 devices: a whole 2x2x4 slice. The times are simulated.
32 devices in a mesh: fsdp: 8 (over z, core), rep: 4 (over y, x).
Axes of the slice: x: 2, y: 2, z: 4, core: 2. Of those that a mesh axis runs over, the one named last changes fastest.
Arguments:
- tokens: bfloat16 [4, 2048, 4096], P('rep', 'fsdp'), may hold values from -6 to 6
- cotangent: bfloat16 [4, 2048, 4096], P('rep', 'fsdp'), may hold values from -1.1953125 to 1.1953125
- block_map: int32 [8, 2], replicated, may hold values from 0 to 31
- matching: int32 [4], replicated, may hold values from 0 to 3, as said below
- tiles: bfloat16 [4, 8, 3, 128, 128], P('rep', 'fsdp'), may hold values from -4 to 4
- first_moment: float32 [4, 8, 3, 128, 128], P('rep', 'fsdp'), may hold values from -3 to 3
- second_moment: float32 [4, 8, 3, 128, 128], P('rep', 'fsdp'), may hold values from 0.3 to 3
Outputs:
- new_tiles: bfloat16 [4, 8, 3, 128, 128], P('rep', 'fsdp')
- new_first: float32 [4, 8, 3, 128, 128], P('rep', 'fsdp')
- new_second: float32 [4, 8, 3, 128, 128], P('rep', 'fsdp')
Inputs may be any that keep to these rules, and one draw needn't show every extreme that they name: `matching`: replica r is paired with replica r XOR k, for one k of 1 to 3 drawn for the step.
All inputs are finite; a program needn't handle non-finite values.
Results may differ from a plain program's by a relative error of at most 0.0055.
Values may be sent and summed in bfloat16 or wider, within the bound.
No kernel may reach another device: no remote copies, remote signals or barrier semaphores. Data moves between devices by JAX's collectives and lax.ppermute only.
A program may use at most 64 MiB of HBM per device.

v0:
```python
import jax
import jax.numpy as jnp
from jax import lax
from jax.sharding import PartitionSpec as P

BETA_ONE = 0.9
BETA_TWO = 0.95
STEP_RATE = 0.02
WEIGHT_DECAY = 0.1
EPSILON = 1e-08


def swapped(value, axis, stride):
    mask = 2**stride
    pairs = [(source, source ^ mask) for source in range(lax.axis_size(axis))]
    return lax.ppermute(value, axis, pairs)


def unit_terms(inputs_a, cots_b, weights):
    tile_edge = weights.shape[-1]
    factor = tile_edge ** (-0.5)
    gate_pre = factor * jnp.einsum(
        "tui,uih->tuh", inputs_a, weights[:, 0], preferred_element_type=jnp.float32
    )
    up_pre = factor * jnp.einsum(
        "tui,uih->tuh", inputs_a, weights[:, 1], preferred_element_type=jnp.float32
    )
    sigmoid = jax.nn.sigmoid(gate_pre)
    activated = gate_pre * sigmoid
    hidden = (activated * up_pre).astype(jnp.bfloat16)
    hidden_grad = factor * jnp.einsum(
        "tuo,uho->tuh", cots_b, weights[:, 2], preferred_element_type=jnp.float32
    )
    gate_grad = (hidden_grad * up_pre * sigmoid * (1.0 + gate_pre * (1.0 - sigmoid))).astype(
        jnp.bfloat16
    )
    up_grad = (hidden_grad * activated).astype(jnp.bfloat16)
    gate_term = factor * jnp.einsum(
        "tui,tuh->uih", inputs_a, gate_grad, preferred_element_type=jnp.float32
    )
    up_term = factor * jnp.einsum(
        "tui,tuh->uih", inputs_a, up_grad, preferred_element_type=jnp.float32
    )
    down_term = factor * jnp.einsum(
        "tuh,tuo->uho", hidden, cots_b, preferred_element_type=jnp.float32
    )
    return jnp.stack([gate_term, up_term, down_term], axis=1)


def pick_blocks(rows, block_ids, tile_edge):
    return jnp.take(rows.reshape(rows.shape[0], -1, tile_edge), block_ids, axis=1)


def body(tokens, cotangent, block_map, matching, tiles, first_moment, second_moment):
    local = tiles[0]
    tile_edge = local.shape[-1]
    own_tokens = tokens[0]
    own_cots = cotangent[0]
    whole = lax.all_gather(local, "fsdp", axis=0, tiled=True)
    inputs_a = pick_blocks(own_tokens, block_map[:, 0], tile_edge)
    cots_b = pick_blocks(own_cots, block_map[:, 1], tile_edge)
    grads = lax.psum_scatter(
        unit_terms(inputs_a, cots_b, whole).astype(jnp.bfloat16),
        "fsdp",
        scatter_dimension=0,
        tiled=True,
    ).astype(jnp.float32)
    offset = matching[0]
    moving = local
    for bit_number in range(lax.axis_size("rep").bit_length() - 1):
        arrived = swapped(moving, "rep", bit_number)
        moving = jnp.where(offset >> bit_number & 1 == 1, arrived, moving)
    weights32 = local.astype(jnp.float32)
    new_first = BETA_ONE * first_moment[0] + (1.0 - BETA_ONE) * grads
    new_second = BETA_TWO * second_moment[0] + (1.0 - BETA_TWO) * grads * grads
    mixed = 0.5 * (weights32 + moving.astype(jnp.float32)) - STEP_RATE * (
        new_first / (jnp.sqrt(new_second) + EPSILON) + WEIGHT_DECAY * weights32
    )
    return (mixed.astype(jnp.bfloat16)[None], new_first[None], new_second[None])


def solution(mesh):
    placed = (
        P("rep", "fsdp", None),
        P("rep", "fsdp", None),
        P(),
        P(),
        P("rep", "fsdp", None, None, None),
        P("rep", "fsdp", None, None, None),
        P("rep", "fsdp", None, None, None),
    )
    return jax.shard_map(
        body,
        mesh=mesh,
        in_specs=placed,
        out_specs=(
            P("rep", "fsdp", None, None, None),
            P("rep", "fsdp", None, None, None),
            P("rep", "fsdp", None, None, None),
        ),
        check_vma=False,
    )
```

profile of v0, /device:TPU:0, one launch (start us, length us, event | category | flops | bytes accessed | tf_op | source)
XLA Modules:
  0.0 117.8 jit_solution(10592363397574259431)
XLA Ops:
  7.2 0.0 all-reduce.3.cloned.1.call-start
  7.2 3.0 %collective-permute-start = (bf16[1,3,128,128]{3,2,0,1:T(8,128)(2,1)}, bf16[1,3,128,128]{3,2,0,1:T(8,128)(2,1)S(1)}, u32[]{:S(2)}, u32[]{:S(2)}) collective-permute-start(bf16[1,3,128,128]{3,2,0,1:T(8,128)(2,1)} %bitcast.85), channel_id=1, source_target_pairs={{0,1},{1,0},{2,3},{3,2},{4,5},{5,4},{6,7},{7,6},{8,9},{9,8},{10,11... | collective-permute-start | bytes 294920 | tf_op jit(solution)/shard_map/ppermute | solution.py:16
  10.2 15.9 %all-gather = bf16[8,1,3,128,128]{4,3,0,2,1:T(8,128)(2,1)S(1)} all-gather(bf16[1,1,3,128,128]{4,3,0,2,1:T(8,128)(2,1)} %bitcast.86), channel_id=2, replica_groups=mesh['fsdp'=8,'rep'=4] {'fsdp'}, dimensions={0}, use_global_device_ids=true | all-gather | bytes 884736 | tf_op jit(solution)/shard_map/all_gather | solution.py:59
  26.2 3.3 %copy.26 = bf16[1,256,4096]{1,2,0:T(8,128)(2,1)S(1)} copy(bf16[1,256,4096]{2,1,0:T(8,128)(2,1)} %param.9) | data formatting | bytes 4194304 | tf_op args[0]
  29.5 0.0 copy-start.5
  29.5 2.9 %copy.27 = bf16[256,32,128]{2,0,1:T(8,128)(2,1)} copy(bf16[256,32,128]{0,2,1:T(8,128)(2,1)S(1)} %bitcast.80) | data formatting | bytes 4194304 | tf_op jit(solution)/shard_map/reshape;squeeze | solution.py:51
  32.4 2.2 %gather_fusion = bf16[8,256,128]{2,1,0:T(8,128)(2,1)S(1)} fusion(bf16[256,32,128]{2,0,1:T(8,128)(2,1)} %copy.27, s32[1024]{0:T(1024)S(1)} %get-tuple-element.14), kind=kCustom, calls=%fused_computation.clone | custom fusion | bytes 1048608 | tf_op jit(solution)/shard_map/jit(_take)/gather | solution.py:51
  34.6 1.3 %fusion.1 = f32[256,8,128]{2,0,1:T(8,128)} fusion(bf16[8,3,128,128]{3,2,0,1:T(8,128)(2,1)S(1)} %bitcast.82, bf16[8,256,128]{2,1,0:T(8,128)(2,1)S(1)} %gather_fusion, pred[8]{0:T(512)(128)(4,1)S(1)} %get-tuple-element.11), kind=kOutput, calls=%fused_computation.5 | convolution fusion | flops 67633152 | bytes 1835520 | tf_op jit(solution)/shard_map/tui,uih->tuh/dot_general | solution.py:25
  35.9 1.4 %fusion = f32[256,8,128]{2,0,1:T(8,128)} fusion(bf16[8,3,128,128]{3,2,0,1:T(8,128)(2,1)S(1)} %bitcast.83, bf16[8,256,128]{2,1,0:T(8,128)(2,1)S(1)} %gather_fusion, pred[8]{0:T(512)(128)(4,1)S(1)} %get-tuple-element.11), kind=kOutput, calls=%fused_computation.3 | convolution fusion | flops 67633152 | bytes 1835520 | tf_op jit(solution)/shard_map/tui,uih->tuh/dot_general | solution.py:22
  37.3 3.3 %copy.28 = bf16[1,256,4096]{1,2,0:T(8,128)(2,1)S(1)} copy(bf16[1,256,4096]{2,1,0:T(8,128)(2,1)} %param.10) | data formatting | bytes 4194304 | tf_op args[1]
  40.6 2.9 %copy.29 = bf16[256,32,128]{2,0,1:T(8,128)(2,1)} copy(bf16[256,32,128]{0,2,1:T(8,128)(2,1)S(1)} %bitcast.81) | data formatting | bytes 4194304 | tf_op jit(solution)/shard_map/reshape;squeeze | solution.py:51
  43.4 2.3 %gather_fusion.1 = bf16[8,256,128]{2,1,0:T(8,128)(2,1)S(1)} fusion(bf16[256,32,128]{2,0,1:T(8,128)(2,1)} %copy.29, s32[1024]{0:T(1024)S(1)} %get-tuple-element.13), kind=kCustom, calls=%fused_computation.1.clone | custom fusion | bytes 1048608 | tf_op jit(solution)/shard_map/jit(_take)/gather | solution.py:51
  45.8 0.3 fusion.2
  46.2 1.8 %fusion.6 = bf16[8,1,128,128]{3,2,0,1:T(8,128)(2,1)S(1)} fusion(f32[256,8,128]{2,0,1:T(8,128)S(1)} %copy-done, bf16[8,256,128]{2,1,0:T(8,128)(2,1)S(1)} %gather_fusion.1, pred[8]{0:T(512)(128)(4,1)S(1)} %get-tuple-element.4, f32[256,8,128]{2,0,1:T(8,128)} %fusion), kind=kOutput, calls=%fused_computation.14 | convolution fusion | flops 69206016 | bytes 2883592 | tf_op jit(solution)/shard_map/tuh,tuo->uho/dot_general | solution.py:44
  48.0 0.6 fusion.7
  48.6 0.8 fusion.8
  49.4 0.0 copy-start.7
  49.4 1.0 pad_maximum_fusion
  50.4 0.0 all-reduce.3.cloned.1.call-update
  50.6 1.6 %collective-permute-start.1 = (bf16[1,3,128,128]{3,2,0,1:T(8,128)(2,1)S(1)}, bf16[1,3,128,128]{3,2,0,1:T(8,128)(2,1)S(1)}, u32[]{:S(2)}, u32[]{:S(2)}) collective-permute-start(bf16[1,3,128,128]{3,2,0,1:T(8,128)(2,1)S(1)} %broadcast_select_fusion.4), channel_id=1, source_target_pairs={{0,2},{1,3},{2,0},{3,1},{4,6},{5,7},{6,4},{7,5},{8,10},{9,11},{10,... | collective-permute-start | bytes 294920 | tf_op jit(solution)/shard_map/ppermute | solution.py:16
  52.2 0.7 dynamic-slice
  52.9 2.8 %collective-permute-done.1 = bf16[1,3,128,128]{3,2,0,1:T(8,128)(2,1)S(1)} collective-permute-done((bf16[1,3,128,128]{3,2,0,1:T(8,128)(2,1)S(1)}, bf16[1,3,128,128]{3,2,0,1:T(8,128)(2,1)S(1)}, u32[]{:S(2)}, u32[]{:S(2)}) %collective-permute-start.1) | collective-permute-done | bytes 98336 | tf_op jit(solution)/shard_map/ppermute | solution.py:16
  55.7 52.8 %all-reduce.3.cloned.1.call-done = bf16[8,3,128,128]{3,2,0,1:T(8,128)(2,1)} async-done(((bf16[8,3,128,128]{3,2,0,1:T(8,128)(2,1)}), bf16[8,3,128,128]{3,2,0,1:T(8,128)(2,1)}) %all-reduce.3.cloned.1.call-update) | async-done | bytes 786448
  108.4 2.5 %fusion.26 = (f32[1,1,3,128,128]{4,3,2,1,0:T(8,128)}, bf16[1,1,3,128,128]{4,3,2,1,0:T(8,128)(2,1)}, f32[1,1,3,128,128]{4,3,2,1,0:T(8,128)}) fusion(f32[1,1,3,128,128]{4,3,2,1,0:T(8,128)S(1)} %copy-done.3, bf16[8,3,128,128]{3,2,0,1:T(8,128)(2,1)} %all-reduce.3.cloned.1.call-done, u32[]{:T(128)} %bitcast.31, f32[1,1,3,128,128]{4,3,2,1,0:T(8,128)S(1)} %copy-done.4, ...), kind=kLoop, calls=%fused_computation.46 | loop fusion | flops 983040 | bytes 1277957 | tf_op jit(solution)/shard_map/broadcast_in_dim | solution.py:79
  (18 shorter events, 0.1 us)
Async XLA Ops:
  7.2 101.3 %all-reduce.3.cloned.1.call-start = ((), (), s32[]{:S(2)}) async-start(), calls=%async_computation | async-start | bytes 1572864
  7.2 43.3 %collective-permute-start = (bf16[1,3,128,128]{3,2,0,1:T(8,128)(2,1)}, bf16[1,3,128,128]{3,2,0,1:T(8,128)(2,1)S(1)}, u32[]{:S(2)}, u32[]{:S(2)}) collective-permute-start(bf16[1,3,128,128]{3,2,0,1:T(8,128)(2,1)} %bitcast.85), channel_id=1, source_target_pairs={{0,1},{1,0},{2,3},{3,2},{4,5},{5,4},{6,7},{7,6},{8,9},{9,8},{10,11... | collective-permute-start | bytes 294920 | tf_op jit(solution)/shard_map/ppermute | solution.py:16
  29.5 2.9 %copy-start.5 = (s32[8,2]{0,1:T(2,128)S(1)}, s32[8,2]{0,1:T(2,128)}, u32[]{:S(2)}) copy-start(s32[8,2]{0,1:T(2,128)} %param.11) | copy-start | bytes 196
  43.4 2.7 %copy-start = (f32[256,8,128]{2,0,1:T(8,128)S(1)}, f32[256,8,128]{2,0,1:T(8,128)}, u32[]{:S(2)}) copy-start(f32[256,8,128]{2,0,1:T(8,128)} %fusion.1) | copy-start | bytes 3145732
  46.1 1.8 %copy-start.1 = (f32[256,8,128]{2,0,1:T(8,128)S(1)}, f32[256,8,128]{2,0,1:T(8,128)}, u32[]{:S(2)}) copy-start(f32[256,8,128]{2,0,1:T(8,128)} %fusion) | copy-start | bytes 3145732
  49.4 1.1 copy-start.6
  49.4 1.1 copy-start.2
  49.4 2.8 %copy-start.7 = (u32[32]{0:T(128)S(1)}, u32[32]{0:T(128)}, u32[]{:S(2)}) copy-start(u32[32]{0:T(128)} %constant.46) | copy-start | bytes 388
  49.4 59.0 %copy-start.3 = (f32[1,1,3,128,128]{4,3,2,1,0:T(8,128)S(1)}, f32[1,1,3,128,128]{4,3,2,1,0:T(8,128)}, u32[]{:S(2)}) copy-start(f32[1,1,3,128,128]{4,3,2,1,0:T(8,128)} %param.15) | copy-start | bytes 589828
  49.4 59.0 %copy-start.4 = (f32[1,1,3,128,128]{4,3,2,1,0:T(8,128)S(1)}, f32[1,1,3,128,128]{4,3,2,1,0:T(8,128)}, u32[]{:S(2)}) copy-start(f32[1,1,3,128,128]{4,3,2,1,0:T(8,128)} %param.14) | copy-start | bytes 589828
  50.6 5.1 %collective-permute-start.1 = (bf16[1,3,128,128]{3,2,0,1:T(8,128)(2,1)S(1)}, bf16[1,3,128,128]{3,2,0,1:T(8,128)(2,1)S(1)}, u32[]{:S(2)}, u32[]{:S(2)}) collective-permute-start(bf16[1,3,128,128]{3,2,0,1:T(8,128)(2,1)S(1)} %broadcast_select_fusion.4), channel_id=1, source_target_pairs={{0,2},{1,3},{2,0},{3,1},{4,6},{5,7},{6,4},{7,5},{8,10},{9,11},{10,... | collective-permute-start | bytes 294920 | tf_op jit(solution)/shard_map/ppermute | solution.py:16
Sparse Core Ops, SparseCore 0:
  50.6 57.7 all-reduce.2
where the time goes:
time: 118 us
  waiting for transfers between devices  55.6 us (47%)
  local copies, waits for them, and re-layouts  17.6 us (15%)
  blocking collectives  15.9 us (13%)
  between operations  14.3 us (12%)
  matrix products  6.23 us (5%)
  starting transfers between devices  4.64 us (4%)
  other arithmetic  3.57 us (3%)
    unnamed x2, waiting for transfers between devices  52.8 us
    all_gather x1, blocking collectives, body(): whole = lax.all_gather(local, 'fsdp', axis=0, tiled=True)  15.9 us
    unnamed x19, local copies, waits for them, and re-layouts  7.25 us
    another operation x2, local copies, waits for them, and re-layouts, pick_blocks(): rows.reshape(rows.shape[0], -1, tile_edge)  5.74 us
    ppermute x2, starting transfers between devices, swapped(): return lax.ppermute(value, axis, pairs)  4.61 us
    gather x2, local copies, waits for them, and re-layouts, pick_blocks(): jnp.take(rows.reshape(rows.shape[0], -1, tile_edge), block_ids, axis=1)  4.56 us
    ppermute x2, waiting for transfers between devices, swapped(): return lax.ppermute(value, axis, pairs)  2.81 us
    broadcast_in_dim x1, other arithmetic, body(): return (mixed.astype(jnp.bfloat16)[None], new_first[None], new_second[None])  2.54 us
  transfers between devices with their start and end apart: 3, of which 2 were waited for; matrix products, arithmetic and copies ran while one was open for 21% of the time, Pallas kernels for 0%

commit v1 on v0

v1 whole, which is shorter than its diff:
```python
import functools

import jax
import jax.numpy as jnp
from jax import lax
from jax.experimental import pallas as pl
from jax.experimental.pallas import tpu as pltpu
from jax.sharding import PartitionSpec as P


BETA_ONE = 0.9
BETA_TWO = 0.95
STEP_RATE = 0.02
WEIGHT_DECAY = 0.1
EPSILON = 1e-08


def exchanged(value, axis, mask):
    pairs = [(source, source ^ mask) for source in range(lax.axis_size(axis))]
    return lax.ppermute(value, axis, pairs)


def pack_kernel(edge, map_ref, tokens_ref, cots_ref, *rest):
    outs, sems = rest[:-1], rest[-1]
    me = lax.axis_index("fsdp")
    copies = []
    for mask, out in enumerate(outs):
        unit = me ^ mask
        for side, source in enumerate((tokens_ref, cots_ref)):
            start = pl.multiple_of(map_ref[side, unit] * edge, edge)
            copies.append(
                pltpu.make_async_copy(
                    source.at[0, :, pl.ds(start, edge)], out.at[side], sems.at[2 * mask + side]
                )
            )
    for copy in copies:
        copy.start()
    for copy in copies:
        copy.wait()


def packed(tokens, cotangent, block_map, edge):
    units = lax.axis_size("fsdp")
    rows = tokens.shape[1]
    return pl.pallas_call(
        functools.partial(pack_kernel, edge),
        out_shape=[jax.ShapeDtypeStruct((2, rows, edge), tokens.dtype)] * units,
        in_specs=[
            pl.BlockSpec(memory_space=pltpu.SMEM),
            pl.BlockSpec(memory_space=pltpu.HBM),
            pl.BlockSpec(memory_space=pltpu.HBM),
        ],
        out_specs=[pl.BlockSpec(memory_space=pltpu.VMEM)] * units,
        scratch_shapes=[pltpu.SemaphoreType.DMA((2 * units,))],
        compiler_params=pltpu.CompilerParams(vmem_limit_bytes=16 * 2**20),
    )(
        pltpu.with_memory_space_constraint(block_map.T, pltpu.HBM),
        pltpu.with_memory_space_constraint(tokens, pltpu.HBM),
        pltpu.with_memory_space_constraint(cotangent, pltpu.HBM),
    )


def run_terms(inputs_a, cots_b, tile_ref):
    factor = inputs_a.shape[-1] ** (-0.5)
    dot = functools.partial(lax.dot_general, preferred_element_type=jnp.float32)
    rows = (((1,), (0,)), ((), ()))
    rows_t = (((1,), (1,)), ((), ()))
    summed = (((0,), (0,)), ((), ()))
    gate_pre = factor * dot(inputs_a, tile_ref[0], rows)
    up_pre = factor * dot(inputs_a, tile_ref[1], rows)
    hidden_grad = factor * dot(cots_b, tile_ref[2], rows_t)
    sigmoid = jax.nn.sigmoid(gate_pre)
    activated = gate_pre * sigmoid
    hidden = (activated * up_pre).astype(jnp.bfloat16)
    gate_grad = (hidden_grad * up_pre * sigmoid * (1.0 + gate_pre * (1.0 - sigmoid))).astype(
        jnp.bfloat16
    )
    up_grad = (hidden_grad * activated).astype(jnp.bfloat16)
    return [
        (factor * dot(inputs_a, gate_grad, summed)).astype(jnp.bfloat16).astype(jnp.float32),
        (factor * dot(inputs_a, up_grad, summed)).astype(jnp.bfloat16).astype(jnp.float32),
        (factor * dot(hidden, cots_b, summed)).astype(jnp.bfloat16).astype(jnp.float32),
    ]


def step_kernel(runs, *refs):
    pieces = refs[:runs]
    tile_ref, partner_ref, first_ref, second_ref, new_tile, new_first, new_second = refs[runs:]
    grads = None
    for piece in pieces:
        terms = run_terms(piece[0], piece[1], tile_ref)
        grads = terms if grads is None else [a + b for a, b in zip(grads, terms)]
    for part, grad in enumerate(grads):
        weights = tile_ref[part].astype(jnp.float32)
        first = BETA_ONE * first_ref[part] + (1.0 - BETA_ONE) * grad
        second = BETA_TWO * second_ref[part] + (1.0 - BETA_TWO) * grad * grad
        mixed = 0.5 * (weights + partner_ref[part].astype(jnp.float32)) - STEP_RATE * (
            first / (jnp.sqrt(second) + EPSILON) + WEIGHT_DECAY * weights
        )
        new_tile[part] = mixed.astype(new_tile.dtype)
        new_first[part] = first
        new_second[part] = second


def body(tokens, cotangent, block_map, matching, tiles, first_moment, second_moment):
    units = lax.axis_size("fsdp")
    tile = tiles[0, 0]
    edge = tile.shape[-1]
    pieces = packed(tokens, cotangent, block_map, edge)
    arrived = [pieces[0]] + [exchanged(pieces[mask], "fsdp", mask) for mask in range(1, units)]
    offset = matching[0]
    partner = tile
    for bit_number in range(lax.axis_size("rep").bit_length() - 1):
        swapped = exchanged(partner, "rep", 2**bit_number)
        partner = jnp.where(offset >> bit_number & 1 == 1, swapped, partner)
    new_tile, new_first, new_second = pl.pallas_call(
        functools.partial(step_kernel, units),
        out_shape=[
            jax.ShapeDtypeStruct(tile.shape, tile.dtype),
            jax.ShapeDtypeStruct(tile.shape, jnp.float32),
            jax.ShapeDtypeStruct(tile.shape, jnp.float32),
        ],
        in_specs=[pl.BlockSpec(memory_space=pltpu.VMEM)] * (units + 4),
        out_specs=[pl.BlockSpec(memory_space=pltpu.VMEM)] * 3,
        compiler_params=pltpu.CompilerParams(vmem_limit_bytes=16 * 2**20),
    )(*arrived, tile, partner, first_moment[0, 0], second_moment[0, 0])
    return new_tile[None, None], new_first[None, None], new_second[None, None]


def solution(mesh):
    wide = P("rep", "fsdp", None)
    deep = P("rep", "fsdp", None, None, None)
    return jax.shard_map(
        body,
        mesh=mesh,
        in_specs=(wide, wide, P(), P(), deep, deep, deep),
        out_specs=(deep, deep, deep),
        check_vma=False,
    )
```

time: 118 us -> 37.8 us (0.32)
  the two profiles are of different devices: /device:TPU:0 before, /device:TPU:17 now
where the time goes in v1:
time: 37.8 us; the launch traced here: 37.6 us
  waiting for transfers between devices  21 us (56%)
  starting transfers between devices  10.5 us (28%)
  Pallas kernels  5.35 us (14%)
  between operations  0.77 us (2%)
    ppermute x9, waiting for transfers between devices, exchanged(): return lax.ppermute(value, axis, pairs)  21 us
    ppermute x9, starting transfers between devices, exchanged(): return lax.ppermute(value, axis, pairs)  10.5 us
    pallas_call x1, Pallas kernels, body(): pl.pallas_call(functools.partial(step_kernel, units), out_shape=[jax.Shap...  3.1 us
    pallas_call x1, Pallas kernels, packed(): pl.pallas_call(functools.partial(pack_kernel, edge), out_shape=[jax.Shape...  2.25 us
  transfers between devices with their start and end apart: 9, of which 5 were waited for; matrix products, arithmetic and copies ran while one was open for 0% of the time, Pallas kernels for 6%

profile of v1, /device:TPU:17, one launch (start us, length us, event | category | flops | bytes accessed | tf_op | source)
XLA Modules:
  0.0 37.6 jit_solution(11088183199981314926)
XLA Ops:
  0.6 1.3 %collective-permute-start.7 = (bf16[3,128,128]{2,1,0:T(8,128)(2,1)}, bf16[3,128,128]{2,1,0:T(8,128)(2,1)S(1)}, u32[]{:S(2)}, u32[]{:S(2)}) collective-permute-start(bf16[3,128,128]{2,1,0:T(8,128)(2,1)} %bitcast.11), channel_id=1, source_target_pairs={{0,1},{1,0},{2,3},{3,2},{4,5},{5,4},{6,7},{7,6},{8,9},{9,8},{10,11... | collective-permute-start | bytes 294920 | tf_op jit(solution)/shard_map/ppermute | solution.py:20
  1.9 2.2 %shard_map.94 = (bf16[2,256,128]{2,1,0:T(8,128)(2,1)S(1)}, bf16[2,256,128]{2,1,0:T(8,128)(2,1)S(1)}, bf16[2,256,128]{2,1,0:T(8,128)(2,1)S(1)}, bf16[2,256,128]{2...) custom-call(s32[2,8]{1,0:T(2,128)} %bitcast.15, ...), custom_call_target="tpu_custom_call" | custom-call | tf_op jit(solution)/shard_map/pallas_call | solution.py:45
  4.2 1.0 %collective-permute-start = (bf16[2,256,128]{2,1,0:T(8,128)(2,1)S(1)}, bf16[2,256,128]{2,1,0:T(8,128)(2,1)S(1)}, u32[]{:S(2)}, u32[]{:S(2)}) collective-permute-start(bf16[2,256,128]{2,1,0:T(8,128)(2,1)S(1)} %get-tuple-element.15), channel_id=1, source_target_pairs={{0,4},{4,0},{8,12},{12,8},{16,20},{20,16},{24,28},{28,24},{1,5},{5... | collective-permute-start | bytes 393224 | tf_op jit(solution)/shard_map/ppermute | solution.py:20
  5.2 1.3 %collective-permute-start.1 = (bf16[2,256,128]{2,1,0:T(8,128)(2,1)S(1)}, bf16[2,256,128]{2,1,0:T(8,128)(2,1)S(1)}, u32[]{:S(2)}, u32[]{:S(2)}) collective-permute-start(bf16[2,256,128]{2,1,0:T(8,128)(2,1)S(1)} %get-tuple-element.16), channel_id=1, source_target_pairs={{0,8},{4,12},{8,0},{12,4},{16,24},{20,28},{24,16},{28,20},{1,9},{5... | collective-permute-start | bytes 393224 | tf_op jit(solution)/shard_map/ppermute | solution.py:20
  6.5 0.0 copy-done.3
  6.5 0.0 collective-permute-done.7
  6.5 0.0 copy-done
  6.6 1.3 %collective-permute-start.8 = (bf16[3,128,128]{2,1,0:T(8,128)(2,1)S(1)}, bf16[3,128,128]{2,1,0:T(8,128)(2,1)S(1)}, u32[]{:S(2)}, u32[]{:S(2)}) collective-permute-start(bf16[3,128,128]{2,1,0:T(8,128)(2,1)S(1)} %broadcast_select_fusion), channel_id=1, source_target_pairs={{0,2},{1,3},{2,0},{3,1},{4,6},{5,7},{6,4},{7,5},{8,10},{9,11},{10,... | collective-permute-start | bytes 294920 | tf_op jit(solution)/shard_map/ppermute | solution.py:20
  7.9 1.1 %collective-permute-start.2 = (bf16[2,256,128]{2,1,0:T(8,128)(2,1)S(1)}, bf16[2,256,128]{2,1,0:T(8,128)(2,1)S(1)}, u32[]{:S(2)}, u32[]{:S(2)}) collective-permute-start(bf16[2,256,128]{2,1,0:T(8,128)(2,1)S(1)} %get-tuple-element.17), channel_id=1, source_target_pairs={{0,12},{4,8},{8,4},{12,0},{16,28},{20,24},{24,20},{28,16},{1,13},{... | collective-permute-start | bytes 393224 | tf_op jit(solution)/shard_map/ppermute | solution.py:20
  9.0 0.1 collective-permute-start.3
  9.1 0.0 collective-permute-done.refs_1_
  9.1 2.1 %collective-permute-start.4 = (bf16[2,256,128]{2,1,0:T(8,128)(2,1)S(1)}, bf16[2,256,128]{2,1,0:T(8,128)(2,1)S(1)}, u32[]{:S(2)}, u32[]{:S(2)}) collective-permute-start(bf16[2,256,128]{2,1,0:T(8,128)(2,1)S(1)} %get-tuple-element.19), channel_id=1, source_target_pairs={{0,20},{4,16},{8,28},{12,24},{16,4},{20,0},{24,12},{28,8},{1,21},{... | collective-permute-start | bytes 393224 | tf_op jit(solution)/shard_map/ppermute | solution.py:20
  11.2 0.0 collective-permute-done.1.refs_2_
  11.2 0.1 collective-permute-start.5
  11.3 0.0 collective-permute-done.8
  11.3 2.2 %collective-permute-start.6 = (bf16[2,256,128]{2,1,0:T(8,128)(2,1)S(1)}, bf16[2,256,128]{2,1,0:T(8,128)(2,1)S(1)}, u32[]{:S(2)}, u32[]{:S(2)}) collective-permute-start(bf16[2,256,128]{2,1,0:T(8,128)(2,1)S(1)} %get-tuple-element.21), channel_id=1, source_target_pairs={{0,28},{4,24},{8,20},{12,16},{16,12},{20,8},{24,4},{28,0},{1,29},{... | collective-permute-start | bytes 393224 | tf_op jit(solution)/shard_map/ppermute | solution.py:20
  13.5 0.5 %collective-permute-done.2.refs_3_ = bf16[2,256,128]{2,1,0:T(8,128)(2,1)S(1)} collective-permute-done((bf16[2,256,128]{2,1,0:T(8,128)(2,1)S(1)}, bf16[2,256,128]{2,1,0:T(8,128)(2,1)S(1)}, u32[]{:S(2)}, u32[]{:S(2)}) %collective-permute-start.2) | collective-permute-done | bytes 131104 | tf_op jit(solution)/shard_map/ppermute | solution.py:20
  14.0 2.0 %collective-permute-done.3.refs_4_ = bf16[2,256,128]{2,1,0:T(8,128)(2,1)S(1)} collective-permute-done((bf16[2,256,128]{2,1,0:T(8,128)(2,1)S(1)}, bf16[2,256,128]{2,1,0:T(8,128)(2,1)S(1)}, u32[]{:S(2)}, u32[]{:S(2)}) %collective-permute-start.3) | collective-permute-done | bytes 131104 | tf_op jit(solution)/shard_map/ppermute | solution.py:20
  15.9 10.4 %collective-permute-done.4.refs_5_ = bf16[2,256,128]{2,1,0:T(8,128)(2,1)S(1)} collective-permute-done((bf16[2,256,128]{2,1,0:T(8,128)(2,1)S(1)}, bf16[2,256,128]{2,1,0:T(8,128)(2,1)S(1)}, u32[]{:S(2)}, u32[]{:S(2)}) %collective-permute-start.4) | collective-permute-done | bytes 131104 | tf_op jit(solution)/shard_map/ppermute | solution.py:20
  26.3 5.3 %collective-permute-done.5.refs_6_ = bf16[2,256,128]{2,1,0:T(8,128)(2,1)S(1)} collective-permute-done((bf16[2,256,128]{2,1,0:T(8,128)(2,1)S(1)}, bf16[2,256,128]{2,1,0:T(8,128)(2,1)S(1)}, u32[]{:S(2)}, u32[]{:S(2)}) %collective-permute-start.5) | collective-permute-done | bytes 131104 | tf_op jit(solution)/shard_map/ppermute | solution.py:20
  31.6 2.8 %collective-permute-done.6.refs_7_ = bf16[2,256,128]{2,1,0:T(8,128)(2,1)S(1)} collective-permute-done((bf16[2,256,128]{2,1,0:T(8,128)(2,1)S(1)}, bf16[2,256,128]{2,1,0:T(8,128)(2,1)S(1)}, u32[]{:S(2)}, u32[]{:S(2)}) %collective-permute-start.6) | collective-permute-done | bytes 131104 | tf_op jit(solution)/shard_map/ppermute | solution.py:20
  34.5 0.0 copy-done.1
  34.5 0.0 copy-done.2
  34.5 3.1 %shard_map.95 = (bf16[3,128,128]{2,1,0:T(8,128)(2,1)}, f32[3,128,128]{2,1,0:T(8,128)}, f32[3,128,128]{2,1,0:T(8,128)}) custom-call(bf16[2,256,128]{2,1,0:T(8,128)(2,1)S(1)} %get-tuple-element.14.refs_0_, bf16[2,256,128]{2,1,0:T(8,128)(2,1)S(1)} %collective-permute-done.refs_1_, bf16[2,256,128]{2,1,0:T(8,128)(2,1)S(1)} %collective-permute-done.1.refs_2_, ...), custom_call_target="tpu_custom_call" | custom-call | tf_op jit(solution)/shard_map/pallas_call | solution.py:116
  (6 shorter events, 0.0 us)
Async XLA Ops:
  0.6 5.9 %collective-permute-start.7 = (bf16[3,128,128]{2,1,0:T(8,128)(2,1)}, bf16[3,128,128]{2,1,0:T(8,128)(2,1)S(1)}, u32[]{:S(2)}, u32[]{:S(2)}) collective-permute-start(bf16[3,128,128]{2,1,0:T(8,128)(2,1)} %bitcast.11), channel_id=1, source_target_pairs={{0,1},{1,0},{2,3},{3,2},{4,5},{5,4},{6,7},{7,6},{8,9},{9,8},{10,11... | collective-permute-start | bytes 294920 | tf_op jit(solution)/shard_map/ppermute | solution.py:20
  1.9 4.6 %copy-start.3 = (s32[4]{0:T(128)S(1)}, s32[4]{0:T(128)}, u32[]{:S(2)}) copy-start(s32[4]{0:T(128)} %param.10) | copy-start | bytes 52
  1.9 4.6 %copy-start = (bf16[1,1,3,128,128]{4,3,2,1,0:T(8,128)(2,1)S(1)}, bf16[1,1,3,128,128]{4,3,2,1,0:T(8,128)(2,1)}, u32[]{:S(2)}) copy-start(bf16[1,1,3,128,128]{4,3,2,1,0:T(8,128)(2,1)} %param.11) | copy-start | bytes 294916
  1.9 32.6 %copy-start.1 = (f32[1,1,3,128,128]{4,3,2,1,0:T(8,128)S(1)}, f32[1,1,3,128,128]{4,3,2,1,0:T(8,128)}, u32[]{:S(2)}) copy-start(f32[1,1,3,128,128]{4,3,2,1,0:T(8,128)} %param.12) | copy-start | bytes 589828
  1.9 32.6 %copy-start.2 = (f32[1,1,3,128,128]{4,3,2,1,0:T(8,128)S(1)}, f32[1,1,3,128,128]{4,3,2,1,0:T(8,128)}, u32[]{:S(2)}) copy-start(f32[1,1,3,128,128]{4,3,2,1,0:T(8,128)} %param.13) | copy-start | bytes 589828
  4.2 4.9 %collective-permute-start = (bf16[2,256,128]{2,1,0:T(8,128)(2,1)S(1)}, bf16[2,256,128]{2,1,0:T(8,128)(2,1)S(1)}, u32[]{:S(2)}, u32[]{:S(2)}) collective-permute-start(bf16[2,256,128]{2,1,0:T(8,128)(2,1)S(1)} %get-tuple-element.15), channel_id=1, source_target_pairs={{0,4},{4,0},{8,12},{12,8},{16,20},{20,16},{24,28},{28,24},{1,5},{5... | collective-permute-start | bytes 393224 | tf_op jit(solution)/shard_map/ppermute | solution.py:20
  5.2 6.0 %collective-permute-start.1 = (bf16[2,256,128]{2,1,0:T(8,128)(2,1)S(1)}, bf16[2,256,128]{2,1,0:T(8,128)(2,1)S(1)}, u32[]{:S(2)}, u32[]{:S(2)}) collective-permute-start(bf16[2,256,128]{2,1,0:T(8,128)(2,1)S(1)} %get-tuple-element.16), channel_id=1, source_target_pairs={{0,8},{4,12},{8,0},{12,4},{16,24},{20,28},{24,16},{28,20},{1,9},{5... | collective-permute-start | bytes 393224 | tf_op jit(solution)/shard_map/ppermute | solution.py:20
  6.6 4.7 %collective-permute-start.8 = (bf16[3,128,128]{2,1,0:T(8,128)(2,1)S(1)}, bf16[3,128,128]{2,1,0:T(8,128)(2,1)S(1)}, u32[]{:S(2)}, u32[]{:S(2)}) collective-permute-start(bf16[3,128,128]{2,1,0:T(8,128)(2,1)S(1)} %broadcast_select_fusion), channel_id=1, source_target_pairs={{0,2},{1,3},{2,0},{3,1},{4,6},{5,7},{6,4},{7,5},{8,10},{9,11},{10,... | collective-permute-start | bytes 294920 | tf_op jit(solution)/shard_map/ppermute | solution.py:20
  7.9 6.1 %collective-permute-start.2 = (bf16[2,256,128]{2,1,0:T(8,128)(2,1)S(1)}, bf16[2,256,128]{2,1,0:T(8,128)(2,1)S(1)}, u32[]{:S(2)}, u32[]{:S(2)}) collective-permute-start(bf16[2,256,128]{2,1,0:T(8,128)(2,1)S(1)} %get-tuple-element.17), channel_id=1, source_target_pairs={{0,12},{4,8},{8,4},{12,0},{16,28},{20,24},{24,20},{28,16},{1,13},{... | collective-permute-start | bytes 393224 | tf_op jit(solution)/shard_map/ppermute | solution.py:20
  9.0 7.0 %collective-permute-start.3 = (bf16[2,256,128]{2,1,0:T(8,128)(2,1)S(1)}, bf16[2,256,128]{2,1,0:T(8,128)(2,1)S(1)}, u32[]{:S(2)}, u32[]{:S(2)}) collective-permute-start(bf16[2,256,128]{2,1,0:T(8,128)(2,1)S(1)} %get-tuple-element.18), channel_id=1, source_target_pairs={{0,16},{4,20},{8,24},{12,28},{16,0},{20,4},{24,8},{28,12},{1,17},{... | collective-permute-start | bytes 393224 | tf_op jit(solution)/shard_map/ppermute | solution.py:20
  9.1 17.2 %collective-permute-start.4 = (bf16[2,256,128]{2,1,0:T(8,128)(2,1)S(1)}, bf16[2,256,128]{2,1,0:T(8,128)(2,1)S(1)}, u32[]{:S(2)}, u32[]{:S(2)}) collective-permute-start(bf16[2,256,128]{2,1,0:T(8,128)(2,1)S(1)} %get-tuple-element.19), channel_id=1, source_target_pairs={{0,20},{4,16},{8,28},{12,24},{16,4},{20,0},{24,12},{28,8},{1,21},{... | collective-permute-start | bytes 393224 | tf_op jit(solution)/shard_map/ppermute | solution.py:20
  11.2 20.4 %collective-permute-start.5 = (bf16[2,256,128]{2,1,0:T(8,128)(2,1)S(1)}, bf16[2,256,128]{2,1,0:T(8,128)(2,1)S(1)}, u32[]{:S(2)}, u32[]{:S(2)}) collective-permute-start(bf16[2,256,128]{2,1,0:T(8,128)(2,1)S(1)} %get-tuple-element.20), channel_id=1, source_target_pairs={{0,24},{4,28},{8,16},{12,20},{16,8},{20,12},{24,0},{28,4},{1,25},{... | collective-permute-start | bytes 393224 | tf_op jit(solution)/shard_map/ppermute | solution.py:20
  11.3 23.2 %collective-permute-start.6 = (bf16[2,256,128]{2,1,0:T(8,128)(2,1)S(1)}, bf16[2,256,128]{2,1,0:T(8,128)(2,1)S(1)}, u32[]{:S(2)}, u32[]{:S(2)}) collective-permute-start(bf16[2,256,128]{2,1,0:T(8,128)(2,1)S(1)} %get-tuple-element.21), channel_id=1, source_target_pairs={{0,28},{4,24},{8,20},{12,16},{16,12},{20,8},{24,4},{28,0},{1,29},{... | collective-permute-start | bytes 393224 | tf_op jit(solution)/shard_map/ppermute | solution.py:20

commit v2 on v1

v2 whole, which is shorter than its diff:
```python
import functools

import jax
import jax.numpy as jnp
from jax import lax
from jax.experimental import pallas as pl
from jax.experimental.pallas import tpu as pltpu
from jax.sharding import PartitionSpec as P


BETA_ONE = 0.9
BETA_TWO = 0.95
STEP_RATE = 0.02
WEIGHT_DECAY = 0.1
EPSILON = 1e-08
GROUP = 4

VMEM_SPEC = pl.BlockSpec(memory_space=pltpu.VMEM)
HBM_SPEC = pl.BlockSpec(memory_space=pltpu.HBM)
SMEM_SPEC = pl.BlockSpec(memory_space=pltpu.SMEM)
KERNEL_PARAMS = pltpu.CompilerParams(vmem_limit_bytes=16 * 2**20)


def exchanged(value, axis, mask):
    pairs = [(source, source ^ mask) for source in range(lax.axis_size(axis))]
    return lax.ppermute(value, axis, pairs)


def kernel_call(*args, **kwargs):
    def call(*operands):
        return pl.pallas_call(*args, compiler_params=KERNEL_PARAMS, **kwargs)(*operands)

    return call


def pack_kernel(edge, masks, map_ref, tokens_ref, cots_ref, *rest):
    outs, sems = rest[:-1], rest[-1]
    me = lax.axis_index("fsdp")
    copies = []
    for place, (mask, out) in enumerate(zip(masks, outs)):
        unit = me ^ mask
        for side, source in enumerate((tokens_ref, cots_ref)):
            start = pl.multiple_of(map_ref[side, unit] * edge, edge)
            copies.append(
                pltpu.make_async_copy(
                    source.at[0, :, pl.ds(start, edge)], out.at[side], sems.at[2 * place + side]
                )
            )
    for copy in copies:
        copy.start()
    for copy in copies:
        copy.wait()


def packed(masks, tokens, cotangent, map_t, edge):
    rows = tokens.shape[1]
    outs = kernel_call(
        functools.partial(pack_kernel, edge, masks),
        out_shape=[jax.ShapeDtypeStruct((2, rows, edge), tokens.dtype)] * len(masks),
        in_specs=[SMEM_SPEC, HBM_SPEC, HBM_SPEC],
        out_specs=[VMEM_SPEC] * len(masks),
        scratch_shapes=[pltpu.SemaphoreType.DMA((2 * len(masks),))],
    )(map_t, tokens, cotangent)
    return dict(zip(masks, outs))


def run_terms(inputs_a, cots_b, tile_ref):
    factor = inputs_a.shape[-1] ** (-0.5)
    dot = functools.partial(lax.dot_general, preferred_element_type=jnp.float32)
    rows = (((1,), (0,)), ((), ()))
    rows_t = (((1,), (1,)), ((), ()))
    summed = (((0,), (0,)), ((), ()))
    gate_pre = factor * dot(inputs_a, tile_ref[0], rows)
    up_pre = factor * dot(inputs_a, tile_ref[1], rows)
    hidden_grad = factor * dot(cots_b, tile_ref[2], rows_t)
    sigmoid = jax.nn.sigmoid(gate_pre)
    activated = gate_pre * sigmoid
    hidden = (activated * up_pre).astype(jnp.bfloat16)
    gate_grad = (hidden_grad * up_pre * sigmoid * (1.0 + gate_pre * (1.0 - sigmoid))).astype(
        jnp.bfloat16
    )
    up_grad = (hidden_grad * activated).astype(jnp.bfloat16)
    return [
        (factor * dot(inputs_a, gate_grad, summed)).astype(jnp.bfloat16).astype(jnp.float32),
        (factor * dot(inputs_a, up_grad, summed)).astype(jnp.bfloat16).astype(jnp.float32),
        (factor * dot(hidden, cots_b, summed)).astype(jnp.bfloat16).astype(jnp.float32),
    ]


def sum_kernel(runs, *refs):
    pieces, tile_ref, before, out = refs[:runs], refs[runs], refs[runs + 1 : -1], refs[-1]
    grads = [before[0][part] for part in range(out.shape[0])] if before else None
    for piece in pieces:
        terms = run_terms(piece[0], piece[1], tile_ref)
        grads = terms if grads is None else [a + b for a, b in zip(grads, terms)]
    for part, grad in enumerate(grads):
        out[part] = grad.astype(out.dtype)


def summed_terms(pieces, tile, before, dtype):
    operands = [*pieces, tile] + ([] if before is None else [before])
    return kernel_call(
        functools.partial(sum_kernel, len(pieces)),
        out_shape=jax.ShapeDtypeStruct(tile.shape, dtype),
        in_specs=[VMEM_SPEC] * len(operands),
        out_specs=VMEM_SPEC,
    )(*operands)


def step_kernel(others, *refs):
    sums = refs[: others + 1]
    tile_ref, partner_ref, first_ref, second_ref, new_tile, new_first, new_second = refs[
        others + 1 :
    ]
    for part in range(tile_ref.shape[0]):
        grad = sums[0][part]
        for other in sums[1:]:
            grad = grad + other[part].astype(jnp.float32)
        weights = tile_ref[part].astype(jnp.float32)
        first = BETA_ONE * first_ref[part] + (1.0 - BETA_ONE) * grad
        second = BETA_TWO * second_ref[part] + (1.0 - BETA_TWO) * grad * grad
        mixed = 0.5 * (weights + partner_ref[part].astype(jnp.float32)) - STEP_RATE * (
            first / (jnp.sqrt(second) + EPSILON) + WEIGHT_DECAY * weights
        )
        new_tile[part] = mixed.astype(new_tile.dtype)
        new_first[part] = first
        new_second[part] = second


def body(tokens, cotangent, block_map, matching, tiles, first_moment, second_moment):
    units = lax.axis_size("fsdp")
    group = min(GROUP, units)
    tile = tiles[0, 0]
    edge = tile.shape[-1]
    hbm = functools.partial(pltpu.with_memory_space_constraint, memory_space=pltpu.HBM)
    sources = (hbm(tokens), hbm(cotangent), hbm(block_map.T), edge)
    pieces = packed(range(units), *sources)

    def gathered(base):
        return [pieces[base]] + [
            exchanged(pieces[base + hop], "fsdp", hop)
            for hop in range(1, group)
        ]

    def reduced(base, weights, dtype):
        runs = gathered(base)
        half = max(1, group // 2)
        early = summed_terms(runs[:half], weights, None, jnp.float32)
        return summed_terms(runs[half:], weights, early, dtype)

    returned = []
    for base in range(group, units, group):
        weights = exchanged(tile, "fsdp", base)
        total = reduced(base, weights, tile.dtype)
        returned.append(exchanged(total, "fsdp", base))
    own = reduced(0, tile, jnp.float32)
    offset = matching[0]
    partner = tile
    for bit_number in range(lax.axis_size("rep").bit_length() - 1):
        swapped = exchanged(partner, "rep", 2**bit_number)
        partner = jnp.where(offset >> bit_number & 1 == 1, swapped, partner)
    operands = [own, *returned, tile, partner, first_moment[0, 0], second_moment[0, 0]]
    new_tile, new_first, new_second = kernel_call(
        functools.partial(step_kernel, len(returned)),
        out_shape=[
            jax.ShapeDtypeStruct(tile.shape, tile.dtype),
            jax.ShapeDtypeStruct(tile.shape, jnp.float32),
            jax.ShapeDtypeStruct(tile.shape, jnp.float32),
        ],
        in_specs=[VMEM_SPEC] * len(operands),
        out_specs=[VMEM_SPEC] * 3,
    )(*operands)
    return new_tile[None, None], new_first[None, None], new_second[None, None]


def solution(mesh):
    wide = P("rep", "fsdp", None)
    deep = P("rep", "fsdp", None, None, None)
    return jax.shard_map(
        body,
        mesh=mesh,
        in_specs=(wide, wide, P(), P(), deep, deep, deep),
        out_specs=(deep, deep, deep),
        check_vma=False,
    )
```

time: 37.8 us -> 30.2 us (0.80)
  the two profiles are of different devices: /device:TPU:17 before, /device:TPU:0 now
where the time goes in v2:
time: 30.2 us; the launch traced here: 30 us
  starting transfers between devices  13.9 us (46%)
  waiting for transfers between devices  9.33 us (31%)
  Pallas kernels  5.96 us (20%)
  between operations  0.82 us (3%)
    ppermute x10, starting transfers between devices, exchanged(): return lax.ppermute(value, axis, pairs)  13.9 us
    ppermute x10, waiting for transfers between devices, exchanged(): return lax.ppermute(value, axis, pairs)  9.33 us
    pallas_call x6, Pallas kernels, call(): pl.pallas_call(*args, compiler_params=KERNEL_PARAMS, **kwargs)(*operands)  5.96 us
  transfers between devices with their start and end apart: 10, of which 5 were waited for; matrix products, arithmetic and copies ran while one was open for 0% of the time, Pallas kernels for 9%

profile of v2, /device:TPU:0, one launch (start us, length us, event | category | flops | bytes accessed | tf_op | source)
XLA Modules:
  0.0 30.0 jit_solution(12384374261154290373)
XLA Ops:
  0.7 2.2 %shard_map.94 = (bf16[2,256,128]{2,1,0:T(8,128)(2,1)S(1)}, bf16[2,256,128]{2,1,0:T(8,128)(2,1)S(1)}, bf16[2,256,128]{2,1,0:T(8,128)(2,1)S(1)}, bf16[2,256,128]{2...) custom-call(s32[2,8]{1,0:T(2,128)} %bitcast.18, ...), custom_call_target="tpu_custom_call" | custom-call | tf_op jit(solution)/shard_map/pallas_call | solution.py:31
  2.9 0.0 copy-start.1
  2.9 0.0 copy-start.2
  2.9 3.1 %collective-permute-start.3 = (bf16[2,256,128]{2,1,0:T(8,128)(2,1)S(1)}, bf16[2,256,128]{2,1,0:T(8,128)(2,1)S(1)}, u32[]{:S(2)}, u32[]{:S(2)}) collective-permute-start(bf16[2,256,128]{2,1,0:T(8,128)(2,1)S(1)} %get-tuple-element.18), channel_id=1, source_target_pairs={{0,8},{4,12},{8,0},{12,4},{16,24},{20,28},{24,16},{28,20},{1,9},{5... | collective-permute-start | bytes 393224 | tf_op jit(solution)/shard_map/ppermute | solution.py:26
  6.1 2.6 %collective-permute-start.5 = (bf16[3,128,128]{2,1,0:T(8,128)(2,1)S(1)}, bf16[3,128,128]{2,1,0:T(8,128)(2,1)S(1)}, u32[]{:S(2)}, u32[]{:S(2)}) collective-permute-start(bf16[3,128,128]{2,1,0:T(8,128)(2,1)S(1)} %bitcast.11), channel_id=1, source_target_pairs={{0,16},{4,20},{8,24},{12,28},{16,0},{20,4},{24,8},{28,12},{1,17},{... | collective-permute-start | bytes 294920 | tf_op jit(solution)/shard_map/ppermute | solution.py:26
  8.6 1.5 %collective-permute-start.8 = (bf16[3,128,128]{2,1,0:T(8,128)(2,1)S(1)}, bf16[3,128,128]{2,1,0:T(8,128)(2,1)S(1)}, u32[]{:S(2)}, u32[]{:S(2)}) collective-permute-start(bf16[3,128,128]{2,1,0:T(8,128)(2,1)S(1)} %bitcast.12), channel_id=1, source_target_pairs={{0,1},{1,0},{2,3},{3,2},{4,5},{5,4},{6,7},{7,6},{8,9},{9,8},{10,11... | collective-permute-start | bytes 294920 | tf_op jit(solution)/shard_map/ppermute | solution.py:26
  10.1 0.4 %collective-permute-start = (bf16[2,256,128]{2,1,0:T(8,128)(2,1)S(1)}, bf16[2,256,128]{2,1,0:T(8,128)(2,1)S(1)}, u32[]{:S(2)}, u32[]{:S(2)}) collective-permute-start(bf16[2,256,128]{2,1,0:T(8,128)(2,1)S(1)} %get-tuple-element.14), channel_id=1, source_target_pairs={{0,8},{4,12},{8,0},{12,4},{16,24},{20,28},{24,16},{28,20},{1,9},{5... | collective-permute-start | bytes 393224 | tf_op jit(solution)/shard_map/ppermute | solution.py:26
  10.6 1.9 %collective-permute-done.5.refs_2_ = bf16[3,128,128]{2,1,0:T(8,128)(2,1)S(1)} collective-permute-done((bf16[3,128,128]{2,1,0:T(8,128)(2,1)S(1)}, bf16[3,128,128]{2,1,0:T(8,128)(2,1)S(1)}, u32[]{:S(2)}, u32[]{:S(2)}) %collective-permute-start.5) | collective-permute-done | bytes 98336 | tf_op jit(solution)/shard_map/ppermute | solution.py:26
  12.5 0.0 collective-permute-start.2
  12.5 0.7 %collective-permute-done.8 = bf16[3,128,128]{2,1,0:T(8,128)(2,1)S(1)} collective-permute-done((bf16[3,128,128]{2,1,0:T(8,128)(2,1)S(1)}, bf16[3,128,128]{2,1,0:T(8,128)(2,1)S(1)}, u32[]{:S(2)}, u32[]{:S(2)}) %collective-permute-start.8) | collective-permute-done | bytes 98336 | tf_op jit(solution)/shard_map/ppermute | solution.py:26
  13.3 2.4 %collective-permute-start.4 = (bf16[2,256,128]{2,1,0:T(8,128)(2,1)S(1)}, bf16[2,256,128]{2,1,0:T(8,128)(2,1)S(1)}, u32[]{:S(2)}, u32[]{:S(2)}) collective-permute-start(bf16[2,256,128]{2,1,0:T(8,128)(2,1)S(1)} %get-tuple-element.19), channel_id=1, source_target_pairs={{0,12},{4,8},{8,4},{12,0},{16,28},{20,24},{24,20},{28,16},{1,13},{... | collective-permute-start | bytes 393224 | tf_op jit(solution)/shard_map/ppermute | solution.py:26
  15.7 0.0 collective-permute-done.3.refs_0_
  15.7 0.0 collective-permute-start.6
  15.7 1.3 %collective-permute-done.6.refs_1_ = bf16[2,256,128]{2,1,0:T(8,128)(2,1)S(1)} collective-permute-done((bf16[2,256,128]{2,1,0:T(8,128)(2,1)S(1)}, bf16[2,256,128]{2,1,0:T(8,128)(2,1)S(1)}, u32[]{:S(2)}, u32[]{:S(2)}) %collective-permute-start.6) | collective-permute-done | bytes 131104 | tf_op jit(solution)/shard_map/ppermute | solution.py:26
  17.0 1.5 %collective-permute-start.9 = (bf16[3,128,128]{2,1,0:T(8,128)(2,1)S(1)}, bf16[3,128,128]{2,1,0:T(8,128)(2,1)S(1)}, u32[]{:S(2)}, u32[]{:S(2)}) collective-permute-start(bf16[3,128,128]{2,1,0:T(8,128)(2,1)S(1)} %broadcast_select_fusion), channel_id=1, source_target_pairs={{0,2},{1,3},{2,0},{3,1},{4,6},{5,7},{6,4},{7,5},{8,10},{9,11},{10,... | collective-permute-start | bytes 294920 | tf_op jit(solution)/shard_map/ppermute | solution.py:26
  18.6 0.7 %shard_map.97.refs_3_ = f32[3,128,128]{2,1,0:T(8,128)S(1)} custom-call(bf16[2,256,128]{2,1,0:T(8,128)(2,1)S(1)} %get-tuple-element.20.refs_0_, bf16[2,256,128]{2,1,0:T(8,128)(2,1)S(1)} %collective-permute-done.6.refs_1_, bf16[3,128,128]{2,1,0:T(8,128)(2,1)S(1)} %collective-permute-done.5.refs_2_), custom_call_target="tpu_custom_call" | custom-call | tf_op jit(solution)/shard_map/pallas_call | solution.py:31
  19.3 0.4 %collective-permute-done.4.refs_1_ = bf16[2,256,128]{2,1,0:T(8,128)(2,1)S(1)} collective-permute-done((bf16[2,256,128]{2,1,0:T(8,128)(2,1)S(1)}, bf16[2,256,128]{2,1,0:T(8,128)(2,1)S(1)}, u32[]{:S(2)}, u32[]{:S(2)}) %collective-permute-start.4) | collective-permute-done | bytes 131104 | tf_op jit(solution)/shard_map/ppermute | solution.py:26
  19.7 0.7 %shard_map.98 = bf16[3,128,128]{2,1,0:T(8,128)(2,1)S(1)} custom-call(bf16[2,256,128]{2,1,0:T(8,128)(2,1)S(1)} %collective-permute-done.3.refs_0_, bf16[2,256,128]{2,1,0:T(8,128)(2,1)S(1)} %collective-permute-done.4.refs_1_, bf16[3,128,128]{2,1,0:T(8,128)(2,1)S(1)} %collective-permute-done.5.refs_2_, f32[3,128,128]{2,1,0:T(8,128)S(1)} %shard_map.97.refs_3_), custom_call_target="tpu_custom_call" | custom-call | tf_op jit(solution)/shard_map/pallas_call | solution.py:31
  20.4 2.3 %collective-permute-start.7 = (bf16[3,128,128]{2,1,0:T(8,128)(2,1)S(1)}, bf16[3,128,128]{2,1,0:T(8,128)(2,1)S(1)}, u32[]{:S(2)}, u32[]{:S(2)}) collective-permute-start(bf16[3,128,128]{2,1,0:T(8,128)(2,1)S(1)} %shard_map.98), channel_id=1, source_target_pairs={{0,16},{4,20},{8,24},{12,28},{16,0},{20,4},{24,8},{28,12},{1,17},{... | collective-permute-start | bytes 294920 | tf_op jit(solution)/shard_map/ppermute | solution.py:26
  22.7 0.0 collective-permute-done.2.refs_1_
  22.7 0.7 %shard_map.95.refs_3_ = f32[3,128,128]{2,1,0:T(8,128)S(1)} custom-call(bf16[2,256,128]{2,1,0:T(8,128)(2,1)S(1)} %get-tuple-element.16.refs_0_, bf16[2,256,128]{2,1,0:T(8,128)(2,1)S(1)} %collective-permute-done.2.refs_1_, bf16[3,128,128]{2,1,0:T(8,128)(2,1)S(1)} %bitcast.13), custom_call_target="tpu_custom_call" | custom-call | tf_op jit(solution)/shard_map/pallas_call | solution.py:31
  23.4 0.7 %shard_map.96.refs_0_ = f32[3,128,128]{2,1,0:T(8,128)S(1)} custom-call(bf16[2,256,128]{2,1,0:T(8,128)(2,1)S(1)} %collective-permute-done.refs_0_, bf16[2,256,128]{2,1,0:T(8,128)(2,1)S(1)} %collective-permute-done.1.refs_1_, bf16[3,128,128]{2,1,0:T(8,128)(2,1)S(1)} %bitcast.14, f32[3,128,128]{2,1,0:T(8,128)S(1)} %shard_map.95.refs_3_), custom_call_target="tpu_custom_call" | custom-call | tf_op jit(solution)/shard_map/pallas_call | solution.py:31
  24.2 4.9 %collective-permute-done.7.refs_1_ = bf16[3,128,128]{2,1,0:T(8,128)(2,1)S(1)} collective-permute-done((bf16[3,128,128]{2,1,0:T(8,128)(2,1)S(1)}, bf16[3,128,128]{2,1,0:T(8,128)(2,1)S(1)}, u32[]{:S(2)}, u32[]{:S(2)}) %collective-permute-start.7) | collective-permute-done | bytes 98336 | tf_op jit(solution)/shard_map/ppermute | solution.py:26
  29.1 0.9 %shard_map.99 = (bf16[3,128,128]{2,1,0:T(8,128)(2,1)}, f32[3,128,128]{2,1,0:T(8,128)}, f32[3,128,128]{2,1,0:T(8,128)}) custom-call(f32[3,128,128]{2,1,0:T(8,128)S(1)} %shard_map.96.refs_0_, bf16[3,128,128]{2,1,0:T(8,128)(2,1)S(1)} %collective-permute-done.7.refs_1_, bf16[3,128,128]{2,1,0:T(8,128)(2,1)S(1)} %bitcast.15, ...), custom_call_target="tpu_custom_call" | custom-call | tf_op jit(solution)/shard_map/pallas_call | solution.py:31
  (12 shorter events, 0.0 us)
Async XLA Ops:
  0.6 5.4 %copy-start = (bf16[1,1,3,128,128]{4,3,2,1,0:T(8,128)(2,1)S(1)}, bf16[1,1,3,128,128]{4,3,2,1,0:T(8,128)(2,1)}, u32[]{:S(2)}) copy-start(bf16[1,1,3,128,128]{4,3,2,1,0:T(8,128)(2,1)} %param.11) | copy-start | bytes 294916
  0.6 9.9 %copy-start.3 = (s32[4]{0:T(128)S(1)}, s32[4]{0:T(128)}, u32[]{:S(2)}) copy-start(s32[4]{0:T(128)} %param.10) | copy-start | bytes 52
  2.9 26.2 %copy-start.1 = (f32[1,1,3,128,128]{4,3,2,1,0:T(8,128)S(1)}, f32[1,1,3,128,128]{4,3,2,1,0:T(8,128)}, u32[]{:S(2)}) copy-start(f32[1,1,3,128,128]{4,3,2,1,0:T(8,128)} %param.12) | copy-start | bytes 589828
  2.9 26.2 %copy-start.2 = (f32[1,1,3,128,128]{4,3,2,1,0:T(8,128)S(1)}, f32[1,1,3,128,128]{4,3,2,1,0:T(8,128)}, u32[]{:S(2)}) copy-start(f32[1,1,3,128,128]{4,3,2,1,0:T(8,128)} %param.13) | copy-start | bytes 589828
  2.9 12.7 %collective-permute-start.3 = (bf16[2,256,128]{2,1,0:T(8,128)(2,1)S(1)}, bf16[2,256,128]{2,1,0:T(8,128)(2,1)S(1)}, u32[]{:S(2)}, u32[]{:S(2)}) collective-permute-start(bf16[2,256,128]{2,1,0:T(8,128)(2,1)S(1)} %get-tuple-element.18), channel_id=1, source_target_pairs={{0,8},{4,12},{8,0},{12,4},{16,24},{20,28},{24,16},{28,20},{1,9},{5... | collective-permute-start | bytes 393224 | tf_op jit(solution)/shard_map/ppermute | solution.py:26
  6.1 6.5 %collective-permute-start.5 = (bf16[3,128,128]{2,1,0:T(8,128)(2,1)S(1)}, bf16[3,128,128]{2,1,0:T(8,128)(2,1)S(1)}, u32[]{:S(2)}, u32[]{:S(2)}) collective-permute-start(bf16[3,128,128]{2,1,0:T(8,128)(2,1)S(1)} %bitcast.11), channel_id=1, source_target_pairs={{0,16},{4,20},{8,24},{12,28},{16,0},{20,4},{24,8},{28,12},{1,17},{... | collective-permute-start | bytes 294920 | tf_op jit(solution)/shard_map/ppermute | solution.py:26
  8.6 4.6 %collective-permute-start.8 = (bf16[3,128,128]{2,1,0:T(8,128)(2,1)S(1)}, bf16[3,128,128]{2,1,0:T(8,128)(2,1)S(1)}, u32[]{:S(2)}, u32[]{:S(2)}) collective-permute-start(bf16[3,128,128]{2,1,0:T(8,128)(2,1)S(1)} %bitcast.12), channel_id=1, source_target_pairs={{0,1},{1,0},{2,3},{3,2},{4,5},{5,4},{6,7},{7,6},{8,9},{9,8},{10,11... | collective-permute-start | bytes 294920 | tf_op jit(solution)/shard_map/ppermute | solution.py:26
  10.1 13.3 %collective-permute-start = (bf16[2,256,128]{2,1,0:T(8,128)(2,1)S(1)}, bf16[2,256,128]{2,1,0:T(8,128)(2,1)S(1)}, u32[]{:S(2)}, u32[]{:S(2)}) collective-permute-start(bf16[2,256,128]{2,1,0:T(8,128)(2,1)S(1)} %get-tuple-element.14), channel_id=1, source_target_pairs={{0,8},{4,12},{8,0},{12,4},{16,24},{20,28},{24,16},{28,20},{1,9},{5... | collective-permute-start | bytes 393224 | tf_op jit(solution)/shard_map/ppermute | solution.py:26
  10.6 12.8 %collective-permute-start.1 = (bf16[2,256,128]{2,1,0:T(8,128)(2,1)S(1)}, bf16[2,256,128]{2,1,0:T(8,128)(2,1)S(1)}, u32[]{:S(2)}, u32[]{:S(2)}) collective-permute-start(bf16[2,256,128]{2,1,0:T(8,128)(2,1)S(1)} %get-tuple-element.15), channel_id=1, source_target_pairs={{0,12},{4,8},{8,4},{12,0},{16,28},{20,24},{24,20},{28,16},{1,13},{... | collective-permute-start | bytes 393224 | tf_op jit(solution)/shard_map/ppermute | solution.py:26
  12.5 10.2 %collective-permute-start.2 = (bf16[2,256,128]{2,1,0:T(8,128)(2,1)S(1)}, bf16[2,256,128]{2,1,0:T(8,128)(2,1)S(1)}, u32[]{:S(2)}, u32[]{:S(2)}) collective-permute-start(bf16[2,256,128]{2,1,0:T(8,128)(2,1)S(1)} %get-tuple-element.17), channel_id=1, source_target_pairs={{0,4},{4,0},{8,12},{12,8},{16,20},{20,16},{24,28},{28,24},{1,5},{5... | collective-permute-start | bytes 393224 | tf_op jit(solution)/shard_map/ppermute | solution.py:26
  13.3 6.4 %collective-permute-start.4 = (bf16[2,256,128]{2,1,0:T(8,128)(2,1)S(1)}, bf16[2,256,128]{2,1,0:T(8,128)(2,1)S(1)}, u32[]{:S(2)}, u32[]{:S(2)}) collective-permute-start(bf16[2,256,128]{2,1,0:T(8,128)(2,1)S(1)} %get-tuple-element.19), channel_id=1, source_target_pairs={{0,12},{4,8},{8,4},{12,0},{16,28},{20,24},{24,20},{28,16},{1,13},{... | collective-permute-start | bytes 393224 | tf_op jit(solution)/shard_map/ppermute | solution.py:26
  15.7 1.3 %collective-permute-start.6 = (bf16[2,256,128]{2,1,0:T(8,128)(2,1)S(1)}, bf16[2,256,128]{2,1,0:T(8,128)(2,1)S(1)}, u32[]{:S(2)}, u32[]{:S(2)}) collective-permute-start(bf16[2,256,128]{2,1,0:T(8,128)(2,1)S(1)} %get-tuple-element.21), channel_id=1, source_target_pairs={{0,4},{4,0},{8,12},{12,8},{16,20},{20,16},{24,28},{28,24},{1,5},{5... | collective-permute-start | bytes 393224 | tf_op jit(solution)/shard_map/ppermute | solution.py:26
  17.0 7.1 %collective-permute-start.9 = (bf16[3,128,128]{2,1,0:T(8,128)(2,1)S(1)}, bf16[3,128,128]{2,1,0:T(8,128)(2,1)S(1)}, u32[]{:S(2)}, u32[]{:S(2)}) collective-permute-start(bf16[3,128,128]{2,1,0:T(8,128)(2,1)S(1)} %broadcast_select_fusion), channel_id=1, source_target_pairs={{0,2},{1,3},{2,0},{3,1},{4,6},{5,7},{6,4},{7,5},{8,10},{9,11},{10,... | collective-permute-start | bytes 294920 | tf_op jit(solution)/shard_map/ppermute | solution.py:26
  20.4 8.7 %collective-permute-start.7 = (bf16[3,128,128]{2,1,0:T(8,128)(2,1)S(1)}, bf16[3,128,128]{2,1,0:T(8,128)(2,1)S(1)}, u32[]{:S(2)}, u32[]{:S(2)}) collective-permute-start(bf16[3,128,128]{2,1,0:T(8,128)(2,1)S(1)} %shard_map.98), channel_id=1, source_target_pairs={{0,16},{4,20},{8,24},{12,28},{16,0},{20,4},{24,8},{28,12},{1,17},{... | collective-permute-start | bytes 294920 | tf_op jit(solution)/shard_map/ppermute | solution.py:26

commit v3 on v2

--- a/solution.py
+++ b/solution.py
@@ -13,6 +13,7 @@
 STEP_RATE = 0.02
 WEIGHT_DECAY = 0.1
 EPSILON = 1e-08
+CORES = 2
 GROUP = 4
 
 VMEM_SPEC = pl.BlockSpec(memory_space=pltpu.VMEM)
@@ -33,46 +34,51 @@
     return call
 
 
-def pack_kernel(edge, masks, map_ref, tokens_ref, cots_ref, *rest):
+def pack_kernel(edge, groups, map_ref, tokens_ref, cots_ref, *rest):
     outs, sems = rest[:-1], rest[-1]
     me = lax.axis_index("fsdp")
     copies = []
-    for place, (mask, out) in enumerate(zip(masks, outs)):
-        unit = me ^ mask
-        for side, source in enumerate((tokens_ref, cots_ref)):
-            start = pl.multiple_of(map_ref[side, unit] * edge, edge)
-            copies.append(
-                pltpu.make_async_copy(
-                    source.at[0, :, pl.ds(start, edge)], out.at[side], sems.at[2 * place + side]
+    for masks, out in zip(groups, outs):
+        for place, mask in enumerate(masks):
+            unit = me ^ mask
+            for side, source in enumerate((tokens_ref, cots_ref)):
+                start = pl.multiple_of(map_ref[side, unit] * edge, edge)
+                copies.append(
+                    pltpu.make_async_copy(
+                        source.at[0, :, pl.ds(start, edge)],
+                        out.at[place, side],
+                        sems.at[len(copies)],
+                    )
                 )
-            )
     for copy in copies:
         copy.start()
     for copy in copies:
         copy.wait()
 
 
-def packed(masks, tokens, cotangent, map_t, edge):
+def packed(groups, tokens, cotangent, map_t, edge):
     rows = tokens.shape[1]
-    outs = kernel_call(
-        functools.partial(pack_kernel, edge, masks),
-        out_shape=[jax.ShapeDtypeStruct((2, rows, edge), tokens.dtype)] * len(masks),
+    return kernel_call(
+        functools.partial(pack_kernel, edge, groups),
+        out_shape=[
+            jax.ShapeDtypeStruct((len(masks), 2, rows, edge), tokens.dtype) for masks in groups
+        ],
         in_specs=[SMEM_SPEC, HBM_SPEC, HBM_SPEC],
-        out_specs=[VMEM_SPEC] * len(masks),
-        scratch_shapes=[pltpu.SemaphoreType.DMA((2 * len(masks),))],
+        out_specs=[VMEM_SPEC] * len(groups),
+        scratch_shapes=[pltpu.SemaphoreType.DMA((2 * sum(map(len, groups)),))],
     )(map_t, tokens, cotangent)
-    return dict(zip(masks, outs))
-
-
-def run_terms(inputs_a, cots_b, tile_ref):
-    factor = inputs_a.shape[-1] ** (-0.5)
+
+
+def run_terms(inputs_a, cots_b, wide_tile, down_tile):
+    edge = inputs_a.shape[-1]
+    factor = edge ** (-0.5)
     dot = functools.partial(lax.dot_general, preferred_element_type=jnp.float32)
     rows = (((1,), (0,)), ((), ()))
     rows_t = (((1,), (1,)), ((), ()))
     summed = (((0,), (0,)), ((), ()))
-    gate_pre = factor * dot(inputs_a, tile_ref[0], rows)
-    up_pre = factor * dot(inputs_a, tile_ref[1], rows)
-    hidden_grad = factor * dot(cots_b, tile_ref[2], rows_t)
+    pre = factor * dot(inputs_a, wide_tile, rows)
+    gate_pre, up_pre = pre[:, :edge], pre[:, edge:]
+    hidden_grad = factor * dot(cots_b, down_tile, rows_t)
     sigmoid = jax.nn.sigmoid(gate_pre)
     activated = gate_pre * sigmoid
     hidden = (activated * up_pre).astype(jnp.bfloat16)
@@ -80,27 +86,29 @@
         jnp.bfloat16
     )
     up_grad = (hidden_grad * activated).astype(jnp.bfloat16)
-    return [
-        (factor * dot(inputs_a, gate_grad, summed)).astype(jnp.bfloat16).astype(jnp.float32),
-        (factor * dot(inputs_a, up_grad, summed)).astype(jnp.bfloat16).astype(jnp.float32),
-        (factor * dot(hidden, cots_b, summed)).astype(jnp.bfloat16).astype(jnp.float32),
-    ]
-
-
-def sum_kernel(runs, *refs):
+    wide_grad = dot(inputs_a, jnp.concatenate([gate_grad, up_grad], axis=1), summed)
+    down_grad = dot(hidden, cots_b, summed)
+    terms = (wide_grad[:, :edge], wide_grad[:, edge:], down_grad)
+    return [(factor * term).astype(jnp.bfloat16).astype(jnp.float32) for term in terms]
+
+
+def sum_kernel(places, *refs):
+    runs = len(places)
     pieces, tile_ref, before, out = refs[:runs], refs[runs], refs[runs + 1 : -1], refs[-1]
     grads = [before[0][part] for part in range(out.shape[0])] if before else None
-    for piece in pieces:
-        terms = run_terms(piece[0], piece[1], tile_ref)
+    wide_tile = jnp.concatenate([tile_ref[0], tile_ref[1]], axis=1)
+    for place, piece in zip(places, pieces):
+        terms = run_terms(piece[place, 0], piece[place, 1], wide_tile, tile_ref[2])
         grads = terms if grads is None else [a + b for a, b in zip(grads, terms)]
     for part, grad in enumerate(grads):
         out[part] = grad.astype(out.dtype)
 
 
-def summed_terms(pieces, tile, before, dtype):
+def summed_terms(runs, tile, before, dtype):
+    pieces, places = zip(*runs)
     operands = [*pieces, tile] + ([] if before is None else [before])
     return kernel_call(
-        functools.partial(sum_kernel, len(pieces)),
+        functools.partial(sum_kernel, places),
         out_shape=jax.ShapeDtypeStruct(tile.shape, dtype),
         in_specs=[VMEM_SPEC] * len(operands),
         out_specs=VMEM_SPEC,
@@ -134,17 +142,30 @@
     edge = tile.shape[-1]
     hbm = functools.partial(pltpu.with_memory_space_constraint, memory_space=pltpu.HBM)
     sources = (hbm(tokens), hbm(cotangent), hbm(block_map.T), edge)
-    pieces = packed(range(units), *sources)
+    cores = min(CORES, units)
+    bases = range(0, units, group)
+    hops = range(cores, group)
+    local = [[base + hop for base in bases] for hop in range(cores)]
+    afar = [[base + hop] for base in bases[1:] for hop in hops]
+    own = [[hop] for hop in hops]
+    first, rest = afar, [*own, *local]
+    groups = [*first, *rest]
+    blocks = packed(first, *sources) if first else []
+    blocks = [*blocks, *packed(rest, *sources)]
+    held = {}
+    for masks, piece in zip(groups, blocks):
+        hop = masks[0] % group
+        if hop:
+            piece = exchanged(piece, "fsdp", hop)
+        for place, mask in enumerate(masks):
+            held[mask] = (piece, place)
 
     def gathered(base):
-        return [pieces[base]] + [
-            exchanged(pieces[base + hop], "fsdp", hop)
-            for hop in range(1, group)
-        ]
+        return [held[base + hop] for hop in range(group)]
 
     def reduced(base, weights, dtype):
         runs = gathered(base)
-        half = max(1, group // 2)
+        half = group - 1
         early = summed_terms(runs[:half], weights, None, jnp.float32)
         return summed_terms(runs[half:], weights, early, dtype)
 

time: 30.2 us -> 30 us (level)
  starting transfers between devices: 13.9 us -> 12.1 us
  Pallas kernels: 5.96 us -> 7.2 us
    ppermute x10 -> x9, starting transfers between devices: 13.9 us -> 12.1 us  [exchanged(): return lax.ppermute(value, axis, pairs)]
    pallas_call x6 -> x7, Pallas kernels: 5.96 us -> 7.2 us  [call(): pl.pallas_call(*args, compiler_params=KERNEL_PARAMS, **kwargs)(*operands)]
    ppermute x10 -> x9, waiting for transfers between devices: 9.33 us -> 9.49 us  [exchanged(): return lax.ppermute(value, axis, pairs)]
  transfers between devices with their start and end apart: 10 -> 9, of which waited for: 5 -> 3; matrix products, arithmetic and copies ran while one was open for 0% -> 0% of each run, Pallas kernels for 9% -> 21%
where the time goes in v3:
time: 30 us; the launch traced here: 29.7 us
  starting transfers between devices  12.1 us (40%)
  waiting for transfers between devices  9.49 us (32%)
  Pallas kernels  7.2 us (24%)
  between operations  0.85 us (3%)
    ppermute x9, starting transfers between devices, exchanged(): return lax.ppermute(value, axis, pairs)  12.1 us
    ppermute x9, waiting for transfers between devices, exchanged(): return lax.ppermute(value, axis, pairs)  9.49 us
    pallas_call x7, Pallas kernels, call(): pl.pallas_call(*args, compiler_params=KERNEL_PARAMS, **kwargs)(*operands)  7.2 us
  transfers between devices with their start and end apart: 9, of which 3 were waited for; matrix products, arithmetic and copies ran while one was open for 0% of the time, Pallas kernels for 21%

profile of v3, /device:TPU:0, one launch (start us, length us, event | category | flops | bytes accessed | tf_op | source)
XLA Modules:
  0.0 29.7 jit_solution(5811845903480586701)
XLA Ops:
  0.6 3.0 %collective-permute-start.7 = (bf16[3,128,128]{2,1,0:T(8,128)(2,1)}, bf16[3,128,128]{2,1,0:T(8,128)(2,1)S(1)}, u32[]{:S(2)}, u32[]{:S(2)}) collective-permute-start(bf16[3,128,128]{2,1,0:T(8,128)(2,1)} %bitcast.11), channel_id=1, source_target_pairs={{0,1},{1,0},{2,3},{3,2},{4,5},{5,4},{6,7},{7,6},{8,9},{9,8},{10,11... | collective-permute-start | bytes 294920 | tf_op jit(solution)/shard_map/ppermute | solution.py:27
  3.7 2.6 %collective-permute-start.4 = (bf16[3,128,128]{2,1,0:T(8,128)(2,1)}, bf16[3,128,128]{2,1,0:T(8,128)(2,1)S(1)}, u32[]{:S(2)}, u32[]{:S(2)}) collective-permute-start(bf16[3,128,128]{2,1,0:T(8,128)(2,1)} %bitcast.12), channel_id=1, source_target_pairs={{0,16},{4,20},{8,24},{12,28},{16,0},{20,4},{24,8},{28,12},{1,17},{... | collective-permute-start | bytes 294920 | tf_op jit(solution)/shard_map/ppermute | solution.py:27
  6.3 2.0 %shard_map.94 = (bf16[1,2,256,128]{3,2,1,0:T(8,128)(2,1)S(1)}, bf16[1,2,256,128]{3,2,1,0:T(8,128)(2,1)S(1)}, bf16[2,2,256,128]{3,2,1,0:T(8,128)(2,1)S(1)}, bf16[2,2,256,128]{3,2,1,0:T(8,128)(2,1)S(1)}) custom-call(s32[2,8]{1,0:T(2,128)} %bitcast.18, bf16[1,256,4096]{2,1,0:T(8,128)(2,1)} %tokens_ref.3, bf16[1,256,4096]{2,1,0:T(8,128)(2,1)} %cots_ref.3), custom_call_target="tpu_custom_call" | custom-call | tf_op jit(solution)/shard_map/pallas_call | solution.py:32
  8.2 0.0 copy-start.3
  8.3 0.0 copy-start
  8.3 0.1 collective-permute-start.1
  8.3 1.7 %shard_map.97 = (bf16[1,2,256,128]{3,2,1,0:T(8,128)(2,1)S(1)}, bf16[1,2,256,128]{3,2,1,0:T(8,128)(2,1)S(1)}) custom-call(s32[2,8]{1,0:T(2,128)} %bitcast.19, bf16[1,256,4096]{2,1,0:T(8,128)(2,1)} %tokens_ref.3, bf16[1,256,4096]{2,1,0:T(8,128)(2,1)} %cots_ref.3), custom_call_target="tpu_custom_call" | custom-call | tf_op jit(solution)/shard_map/pallas_call | solution.py:32
  10.0 0.0 copy-start.1
  10.0 0.0 copy-start.2
  10.1 1.7 %collective-permute-start.3 = (bf16[1,2,256,128]{3,2,1,0:T(8,128)(2,1)S(1)}, bf16[1,2,256,128]{3,2,1,0:T(8,128)(2,1)S(1)}, u32[]{:S(2)}, u32[]{:S(2)}) collective-permute-start(bf16[1,2,256,128]{3,2,1,0:T(8,128)(2,1)S(1)} %get-tuple-element.16), channel_id=1, source_target_pairs={{0,12},{4,8},{8,4},{12,0},{16,28},{20,24},{24,20},{28,16},{1,13},{... | collective-permute-start | bytes 393224 | tf_op jit(solution)/shard_map/ppermute | solution.py:27
  11.8 0.4 %collective-permute-start.5 = (bf16[1,2,256,128]{3,2,1,0:T(8,128)(2,1)S(1)}, bf16[1,2,256,128]{3,2,1,0:T(8,128)(2,1)S(1)}, u32[]{:S(2)}, u32[]{:S(2)}) collective-permute-start(bf16[1,2,256,128]{3,2,1,0:T(8,128)(2,1)S(1)} %get-tuple-element.17), channel_id=1, source_target_pairs={{0,8},{4,12},{8,0},{12,4},{16,24},{20,28},{24,16},{28,20},{1,9},{5... | collective-permute-start | bytes 393224 | tf_op jit(solution)/shard_map/ppermute | solution.py:27
  12.3 0.0 collective-permute-done.7
  12.3 1.6 %collective-permute-start.8 = (bf16[3,128,128]{2,1,0:T(8,128)(2,1)S(1)}, bf16[3,128,128]{2,1,0:T(8,128)(2,1)S(1)}, u32[]{:S(2)}, u32[]{:S(2)}) collective-permute-start(bf16[3,128,128]{2,1,0:T(8,128)(2,1)S(1)} %broadcast_select_fusion), channel_id=1, source_target_pairs={{0,2},{1,3},{2,0},{3,1},{4,6},{5,7},{6,4},{7,5},{8,10},{9,11},{10,... | collective-permute-start | bytes 294920 | tf_op jit(solution)/shard_map/ppermute | solution.py:27
  14.0 0.7 %collective-permute-start = (bf16[1,2,256,128]{3,2,1,0:T(8,128)(2,1)S(1)}, bf16[1,2,256,128]{3,2,1,0:T(8,128)(2,1)S(1)}, u32[]{:S(2)}, u32[]{:S(2)}) collective-permute-start(bf16[1,2,256,128]{3,2,1,0:T(8,128)(2,1)S(1)} %get-tuple-element.12), channel_id=1, source_target_pairs={{0,12},{4,8},{8,4},{12,0},{16,28},{20,24},{24,20},{28,16},{1,13},{... | collective-permute-start | bytes 393224 | tf_op jit(solution)/shard_map/ppermute | solution.py:27
  14.7 4.7 %collective-permute-done.5.refs_2_ = bf16[1,2,256,128]{3,2,1,0:T(8,128)(2,1)S(1)} collective-permute-done((bf16[1,2,256,128]{3,2,1,0:T(8,128)(2,1)S(1)}, bf16[1,2,256,128]{3,2,1,0:T(8,128)(2,1)S(1)}, u32[]{:S(2)}, u32[]{:S(2)}) %collective-permute-start.5) | collective-permute-done | bytes 131104 | tf_op jit(solution)/shard_map/ppermute | solution.py:27
  19.4 1.6 %collective-permute-start.2 = (bf16[1,2,256,128]{3,2,1,0:T(8,128)(2,1)S(1)}, bf16[1,2,256,128]{3,2,1,0:T(8,128)(2,1)S(1)}, u32[]{:S(2)}, u32[]{:S(2)}) collective-permute-start(bf16[1,2,256,128]{3,2,1,0:T(8,128)(2,1)S(1)} %get-tuple-element.15), channel_id=1, source_target_pairs={{0,8},{4,12},{8,0},{12,4},{16,24},{20,28},{24,16},{28,20},{1,9},{5... | collective-permute-start | bytes 393224 | tf_op jit(solution)/shard_map/ppermute | solution.py:27
  21.0 0.9 %shard_map.98.refs_2_ = f32[3,128,128]{2,1,0:T(8,128)S(1)} custom-call(bf16[2,2,256,128]{3,2,1,0:T(8,128)(2,1)S(1)} %get-tuple-element.13.refs_0_, bf16[2,2,256,128]{3,2,1,0:T(8,128)(2,1)S(1)} %collective-permute-done.1.refs_1_, bf16[1,2,256,128]{3,2,1,0:T(8,128)(2,1)S(1)} %collective-permute-done.5.refs_2_, ...), custom_call_target="tpu_custom_call" | custom-call | tf_op jit(solution)/shard_map/pallas_call | solution.py:32
  21.9 0.4 %shard_map.99 = bf16[3,128,128]{2,1,0:T(8,128)(2,1)S(1)} custom-call(bf16[1,2,256,128]{3,2,1,0:T(8,128)(2,1)S(1)} %collective-permute-done.3.refs_0_, bf16[3,128,128]{2,1,0:T(8,128)(2,1)S(1)} %collective-permute-done.4.refs_3_.refs_1_, f32[3,128,128]{2,1,0:T(8,128)S(1)} %shard_map.98.refs_2_), custom_call_target="tpu_custom_call" | custom-call | tf_op jit(solution)/shard_map/pallas_call | solution.py:32
  22.3 0.4 %collective-permute-start.6 = (bf16[3,128,128]{2,1,0:T(8,128)(2,1)S(1)}, bf16[3,128,128]{2,1,0:T(8,128)(2,1)S(1)}, u32[]{:S(2)}, u32[]{:S(2)}) collective-permute-start(bf16[3,128,128]{2,1,0:T(8,128)(2,1)S(1)} %shard_map.99), channel_id=1, source_target_pairs={{0,16},{4,20},{8,24},{12,28},{16,0},{20,4},{24,8},{28,12},{1,17},{... | collective-permute-start | bytes 294920 | tf_op jit(solution)/shard_map/ppermute | solution.py:27
  22.7 1.8 %collective-permute-done.2.refs_2_ = bf16[1,2,256,128]{3,2,1,0:T(8,128)(2,1)S(1)} collective-permute-done((bf16[1,2,256,128]{3,2,1,0:T(8,128)(2,1)S(1)}, bf16[1,2,256,128]{3,2,1,0:T(8,128)(2,1)S(1)}, u32[]{:S(2)}, u32[]{:S(2)}) %collective-permute-start.2) | collective-permute-done | bytes 131104 | tf_op jit(solution)/shard_map/ppermute | solution.py:27
  24.5 0.9 %shard_map.95.refs_2_ = f32[3,128,128]{2,1,0:T(8,128)S(1)} custom-call(bf16[2,2,256,128]{3,2,1,0:T(8,128)(2,1)S(1)} %get-tuple-element.13.refs_0_, bf16[2,2,256,128]{3,2,1,0:T(8,128)(2,1)S(1)} %collective-permute-done.1.refs_1_, bf16[1,2,256,128]{3,2,1,0:T(8,128)(2,1)S(1)} %collective-permute-done.2.refs_2_, bf16[3,128,128]{2,1,0:T(8,128)(2,1)S(1)} %bitcast.13), custom_call_target="tpu_custom_call" | custom-call | tf_op jit(solution)/shard_map/pallas_call | solution.py:32
  25.4 0.4 %shard_map.96.refs_0_ = f32[3,128,128]{2,1,0:T(8,128)S(1)} custom-call(bf16[1,2,256,128]{3,2,1,0:T(8,128)(2,1)S(1)} %collective-permute-done.refs_0_, bf16[3,128,128]{2,1,0:T(8,128)(2,1)S(1)} %bitcast.14, f32[3,128,128]{2,1,0:T(8,128)S(1)} %shard_map.95.refs_2_), custom_call_target="tpu_custom_call" | custom-call | tf_op jit(solution)/shard_map/pallas_call | solution.py:32
  25.8 3.0 %collective-permute-done.6.refs_1_ = bf16[3,128,128]{2,1,0:T(8,128)(2,1)S(1)} collective-permute-done((bf16[3,128,128]{2,1,0:T(8,128)(2,1)S(1)}, bf16[3,128,128]{2,1,0:T(8,128)(2,1)S(1)}, u32[]{:S(2)}, u32[]{:S(2)}) %collective-permute-start.6) | collective-permute-done | bytes 98336 | tf_op jit(solution)/shard_map/ppermute | solution.py:27
  28.8 0.9 %shard_map.100 = (bf16[3,128,128]{2,1,0:T(8,128)(2,1)}, f32[3,128,128]{2,1,0:T(8,128)}, f32[3,128,128]{2,1,0:T(8,128)}) custom-call(f32[3,128,128]{2,1,0:T(8,128)S(1)} %shard_map.96.refs_0_, bf16[3,128,128]{2,1,0:T(8,128)(2,1)S(1)} %collective-permute-done.6.refs_1_, bf16[3,128,128]{2,1,0:T(8,128)(2,1)S(1)} %bitcast.15, ...), custom_call_target="tpu_custom_call" | custom-call | tf_op jit(solution)/shard_map/pallas_call | solution.py:32
  (11 shorter events, 0.0 us)
Async XLA Ops:
  0.6 11.7 %collective-permute-start.7 = (bf16[3,128,128]{2,1,0:T(8,128)(2,1)}, bf16[3,128,128]{2,1,0:T(8,128)(2,1)S(1)}, u32[]{:S(2)}, u32[]{:S(2)}) collective-permute-start(bf16[3,128,128]{2,1,0:T(8,128)(2,1)} %bitcast.11), channel_id=1, source_target_pairs={{0,1},{1,0},{2,3},{3,2},{4,5},{5,4},{6,7},{7,6},{8,9},{9,8},{10,11... | collective-permute-start | bytes 294920 | tf_op jit(solution)/shard_map/ppermute | solution.py:27
  3.7 10.3 %collective-permute-start.4 = (bf16[3,128,128]{2,1,0:T(8,128)(2,1)}, bf16[3,128,128]{2,1,0:T(8,128)(2,1)S(1)}, u32[]{:S(2)}, u32[]{:S(2)}) collective-permute-start(bf16[3,128,128]{2,1,0:T(8,128)(2,1)} %bitcast.12), channel_id=1, source_target_pairs={{0,16},{4,20},{8,24},{12,28},{16,0},{20,4},{24,8},{28,12},{1,17},{... | collective-permute-start | bytes 294920 | tf_op jit(solution)/shard_map/ppermute | solution.py:27
  8.2 4.0 %copy-start.3 = (s32[4]{0:T(128)S(1)}, s32[4]{0:T(128)}, u32[]{:S(2)}) copy-start(s32[4]{0:T(128)} %param.10) | copy-start | bytes 52
  8.3 4.0 %copy-start = (bf16[1,1,3,128,128]{4,3,2,1,0:T(8,128)(2,1)S(1)}, bf16[1,1,3,128,128]{4,3,2,1,0:T(8,128)(2,1)}, u32[]{:S(2)}) copy-start(bf16[1,1,3,128,128]{4,3,2,1,0:T(8,128)(2,1)} %param.11) | copy-start | bytes 294916
  8.3 12.7 %collective-permute-start.1 = (bf16[2,2,256,128]{3,2,1,0:T(8,128)(2,1)S(1)}, bf16[2,2,256,128]{3,2,1,0:T(8,128)(2,1)S(1)}, u32[]{:S(2)}, u32[]{:S(2)}) collective-permute-start(bf16[2,2,256,128]{3,2,1,0:T(8,128)(2,1)S(1)} %get-tuple-element.14), channel_id=1, source_target_pairs={{0,4},{4,0},{8,12},{12,8},{16,20},{20,16},{24,28},{28,24},{1,5},{5... | collective-permute-start | bytes 786440 | tf_op jit(solution)/shard_map/ppermute | solution.py:27
  10.0 18.8 %copy-start.1 = (f32[1,1,3,128,128]{4,3,2,1,0:T(8,128)S(1)}, f32[1,1,3,128,128]{4,3,2,1,0:T(8,128)}, u32[]{:S(2)}) copy-start(f32[1,1,3,128,128]{4,3,2,1,0:T(8,128)} %param.12) | copy-start | bytes 589828
  10.0 18.8 %copy-start.2 = (f32[1,1,3,128,128]{4,3,2,1,0:T(8,128)S(1)}, f32[1,1,3,128,128]{4,3,2,1,0:T(8,128)}, u32[]{:S(2)}) copy-start(f32[1,1,3,128,128]{4,3,2,1,0:T(8,128)} %param.13) | copy-start | bytes 589828
  10.1 11.8 %collective-permute-start.3 = (bf16[1,2,256,128]{3,2,1,0:T(8,128)(2,1)S(1)}, bf16[1,2,256,128]{3,2,1,0:T(8,128)(2,1)S(1)}, u32[]{:S(2)}, u32[]{:S(2)}) collective-permute-start(bf16[1,2,256,128]{3,2,1,0:T(8,128)(2,1)S(1)} %get-tuple-element.16), channel_id=1, source_target_pairs={{0,12},{4,8},{8,4},{12,0},{16,28},{20,24},{24,20},{28,16},{1,13},{... | collective-permute-start | bytes 393224 | tf_op jit(solution)/shard_map/ppermute | solution.py:27
  11.8 7.6 %collective-permute-start.5 = (bf16[1,2,256,128]{3,2,1,0:T(8,128)(2,1)S(1)}, bf16[1,2,256,128]{3,2,1,0:T(8,128)(2,1)S(1)}, u32[]{:S(2)}, u32[]{:S(2)}) collective-permute-start(bf16[1,2,256,128]{3,2,1,0:T(8,128)(2,1)S(1)} %get-tuple-element.17), channel_id=1, source_target_pairs={{0,8},{4,12},{8,0},{12,4},{16,24},{20,28},{24,16},{28,20},{1,9},{5... | collective-permute-start | bytes 393224 | tf_op jit(solution)/shard_map/ppermute | solution.py:27
  12.3 10.4 %collective-permute-start.8 = (bf16[3,128,128]{2,1,0:T(8,128)(2,1)S(1)}, bf16[3,128,128]{2,1,0:T(8,128)(2,1)S(1)}, u32[]{:S(2)}, u32[]{:S(2)}) collective-permute-start(bf16[3,128,128]{2,1,0:T(8,128)(2,1)S(1)} %broadcast_select_fusion), channel_id=1, source_target_pairs={{0,2},{1,3},{2,0},{3,1},{4,6},{5,7},{6,4},{7,5},{8,10},{9,11},{10,... | collective-permute-start | bytes 294920 | tf_op jit(solution)/shard_map/ppermute | solution.py:27
  14.0 11.5 %collective-permute-start = (bf16[1,2,256,128]{3,2,1,0:T(8,128)(2,1)S(1)}, bf16[1,2,256,128]{3,2,1,0:T(8,128)(2,1)S(1)}, u32[]{:S(2)}, u32[]{:S(2)}) collective-permute-start(bf16[1,2,256,128]{3,2,1,0:T(8,128)(2,1)S(1)} %get-tuple-element.12), channel_id=1, source_target_pairs={{0,12},{4,8},{8,4},{12,0},{16,28},{20,24},{24,20},{28,16},{1,13},{... | collective-permute-start | bytes 393224 | tf_op jit(solution)/shard_map/ppermute | solution.py:27
  19.4 5.1 %collective-permute-start.2 = (bf16[1,2,256,128]{3,2,1,0:T(8,128)(2,1)S(1)}, bf16[1,2,256,128]{3,2,1,0:T(8,128)(2,1)S(1)}, u32[]{:S(2)}, u32[]{:S(2)}) collective-permute-start(bf16[1,2,256,128]{3,2,1,0:T(8,128)(2,1)S(1)} %get-tuple-element.15), channel_id=1, source_target_pairs={{0,8},{4,12},{8,0},{12,4},{16,24},{20,28},{24,16},{28,20},{1,9},{5... | collective-permute-start | bytes 393224 | tf_op jit(solution)/shard_map/ppermute | solution.py:27
  22.3 6.5 %collective-permute-start.6 = (bf16[3,128,128]{2,1,0:T(8,128)(2,1)S(1)}, bf16[3,128,128]{2,1,0:T(8,128)(2,1)S(1)}, u32[]{:S(2)}, u32[]{:S(2)}) collective-permute-start(bf16[3,128,128]{2,1,0:T(8,128)(2,1)S(1)} %shard_map.99), channel_id=1, source_target_pairs={{0,16},{4,20},{8,24},{12,28},{16,0},{20,4},{24,8},{28,12},{1,17},{... | collective-permute-start | bytes 294920 | tf_op jit(solution)/shard_map/ppermute | solution.py:27

commit v4 on v3

--- a/solution.py
+++ b/solution.py
@@ -89,19 +89,23 @@
     wide_grad = dot(inputs_a, jnp.concatenate([gate_grad, up_grad], axis=1), summed)
     down_grad = dot(hidden, cots_b, summed)
     terms = (wide_grad[:, :edge], wide_grad[:, edge:], down_grad)
-    return [(factor * term).astype(jnp.bfloat16).astype(jnp.float32) for term in terms]
+    return list(terms)
 
 
 def sum_kernel(places, *refs):
     runs = len(places)
     pieces, tile_ref, before, out = refs[:runs], refs[runs], refs[runs + 1 : -1], refs[-1]
-    grads = [before[0][part] for part in range(out.shape[0])] if before else None
+    factor = tile_ref.shape[-1] ** (-0.5)
+    grads = None
     wide_tile = jnp.concatenate([tile_ref[0], tile_ref[1]], axis=1)
     for place, piece in zip(places, pieces):
         terms = run_terms(piece[place, 0], piece[place, 1], wide_tile, tile_ref[2])
         grads = terms if grads is None else [a + b for a, b in zip(grads, terms)]
     for part, grad in enumerate(grads):
-        out[part] = grad.astype(out.dtype)
+        total = factor * grad
+        if before:
+            total = total + before[0][part]
+        out[part] = total.astype(out.dtype)
 
 
 def summed_terms(runs, tile, before, dtype):
@@ -117,9 +121,10 @@
 
 def step_kernel(others, *refs):
     sums = refs[: others + 1]
-    tile_ref, partner_ref, first_ref, second_ref, new_tile, new_first, new_second = refs[
-        others + 1 :
-    ]
+    tile_ref, partner_ref, first_ref, second_ref = refs[others + 1 : others + 5]
+    targets = refs[others + 5 : others + 8]
+    held, sems = refs[others + 8 : others + 11], refs[others + 11]
+    copies = []
     for part in range(tile_ref.shape[0]):
         grad = sums[0][part]
         for other in sums[1:]:
@@ -130,9 +135,15 @@
         mixed = 0.5 * (weights + partner_ref[part].astype(jnp.float32)) - STEP_RATE * (
             first / (jnp.sqrt(second) + EPSILON) + WEIGHT_DECAY * weights
         )
-        new_tile[part] = mixed.astype(new_tile.dtype)
-        new_first[part] = first
-        new_second[part] = second
+        for place, value in enumerate((mixed.astype(tile_ref.dtype), first, second)):
+            held[place][part] = value
+            copy = pltpu.make_async_copy(
+                held[place].at[part], targets[place].at[part], sems.at[place, part]
+            )
+            copy.start()
+            copies.append(copy)
+    for copy in copies:
+        copy.wait()
 
 
 def body(tokens, cotangent, block_map, matching, tiles, first_moment, second_moment):
@@ -189,7 +200,13 @@
             jax.ShapeDtypeStruct(tile.shape, jnp.float32),
         ],
         in_specs=[VMEM_SPEC] * len(operands),
-        out_specs=[VMEM_SPEC] * 3,
+        out_specs=[HBM_SPEC] * 3,
+        scratch_shapes=[
+            pltpu.VMEM(tile.shape, tile.dtype),
+            pltpu.VMEM(tile.shape, jnp.float32),
+            pltpu.VMEM(tile.shape, jnp.float32),
+            pltpu.SemaphoreType.DMA((3, tile.shape[0])),
+        ],
     )(*operands)
     return new_tile[None, None], new_first[None, None], new_second[None, None]
 

time: 30 us -> 30 us (level)
  no operation moved by 1% of the time
where the time goes in v4:
time: 30 us; the launch traced here: 29.7 us
  starting transfers between devices  12.1 us (40%)
  waiting for transfers between devices  9.58 us (32%)
  Pallas kernels  7.06 us (24%)
  between operations  0.85 us (3%)
    ppermute x9, starting transfers between devices, exchanged(): return lax.ppermute(value, axis, pairs)  12.1 us
    ppermute x9, waiting for transfers between devices, exchanged(): return lax.ppermute(value, axis, pairs)  9.58 us
    pallas_call x7, Pallas kernels, call(): pl.pallas_call(*args, compiler_params=KERNEL_PARAMS, **kwargs)(*operands)  7.06 us
  transfers between devices with their start and end apart: 9, of which 3 were waited for; matrix products, arithmetic and copies ran while one was open for 0% of the time, Pallas kernels for 21%

profile of v4, /device:TPU:0, one launch (start us, length us, event | category | flops | bytes accessed | tf_op | source)
XLA Modules:
  0.0 29.7 jit_solution(451412236005235645)
XLA Ops:
  0.6 3.0 %collective-permute-start.7 = (bf16[3,128,128]{2,1,0:T(8,128)(2,1)}, bf16[3,128,128]{2,1,0:T(8,128)(2,1)S(1)}, u32[]{:S(2)}, u32[]{:S(2)}) collective-permute-start(bf16[3,128,128]{2,1,0:T(8,128)(2,1)} %bitcast.11), channel_id=1, source_target_pairs={{0,1},{1,0},{2,3},{3,2},{4,5},{5,4},{6,7},{7,6},{8,9},{9,8},{10,11... | collective-permute-start | bytes 294920 | tf_op jit(solution)/shard_map/ppermute | solution.py:27
  3.7 2.6 %collective-permute-start.4 = (bf16[3,128,128]{2,1,0:T(8,128)(2,1)}, bf16[3,128,128]{2,1,0:T(8,128)(2,1)S(1)}, u32[]{:S(2)}, u32[]{:S(2)}) collective-permute-start(bf16[3,128,128]{2,1,0:T(8,128)(2,1)} %bitcast.12), channel_id=1, source_target_pairs={{0,16},{4,20},{8,24},{12,28},{16,0},{20,4},{24,8},{28,12},{1,17},{... | collective-permute-start | bytes 294920 | tf_op jit(solution)/shard_map/ppermute | solution.py:27
  6.3 2.0 %shard_map.94 = (bf16[1,2,256,128]{3,2,1,0:T(8,128)(2,1)S(1)}, bf16[1,2,256,128]{3,2,1,0:T(8,128)(2,1)S(1)}, bf16[2,2,256,128]{3,2,1,0:T(8,128)(2,1)S(1)}, bf16[2,2,256,128]{3,2,1,0:T(8,128)(2,1)S(1)}) custom-call(s32[2,8]{1,0:T(2,128)} %bitcast.18, bf16[1,256,4096]{2,1,0:T(8,128)(2,1)} %tokens_ref.3, bf16[1,256,4096]{2,1,0:T(8,128)(2,1)} %cots_ref.3), custom_call_target="tpu_custom_call" | custom-call | tf_op jit(solution)/shard_map/pallas_call | solution.py:32
  8.2 0.0 copy-start.3
  8.3 0.0 copy-start
  8.3 0.1 collective-permute-start.1
  8.3 1.7 %shard_map.97 = (bf16[1,2,256,128]{3,2,1,0:T(8,128)(2,1)S(1)}, bf16[1,2,256,128]{3,2,1,0:T(8,128)(2,1)S(1)}) custom-call(s32[2,8]{1,0:T(2,128)} %bitcast.19, bf16[1,256,4096]{2,1,0:T(8,128)(2,1)} %tokens_ref.3, bf16[1,256,4096]{2,1,0:T(8,128)(2,1)} %cots_ref.3), custom_call_target="tpu_custom_call" | custom-call | tf_op jit(solution)/shard_map/pallas_call | solution.py:32
  10.0 0.0 copy-start.1
  10.0 0.0 copy-start.2
  10.1 1.7 %collective-permute-start.3 = (bf16[1,2,256,128]{3,2,1,0:T(8,128)(2,1)S(1)}, bf16[1,2,256,128]{3,2,1,0:T(8,128)(2,1)S(1)}, u32[]{:S(2)}, u32[]{:S(2)}) collective-permute-start(bf16[1,2,256,128]{3,2,1,0:T(8,128)(2,1)S(1)} %get-tuple-element.16), channel_id=1, source_target_pairs={{0,12},{4,8},{8,4},{12,0},{16,28},{20,24},{24,20},{28,16},{1,13},{... | collective-permute-start | bytes 393224 | tf_op jit(solution)/shard_map/ppermute | solution.py:27
  11.8 0.4 %collective-permute-start.5 = (bf16[1,2,256,128]{3,2,1,0:T(8,128)(2,1)S(1)}, bf16[1,2,256,128]{3,2,1,0:T(8,128)(2,1)S(1)}, u32[]{:S(2)}, u32[]{:S(2)}) collective-permute-start(bf16[1,2,256,128]{3,2,1,0:T(8,128)(2,1)S(1)} %get-tuple-element.17), channel_id=1, source_target_pairs={{0,8},{4,12},{8,0},{12,4},{16,24},{20,28},{24,16},{28,20},{1,9},{5... | collective-permute-start | bytes 393224 | tf_op jit(solution)/shard_map/ppermute | solution.py:27
  12.3 0.0 collective-permute-done.7
  12.3 1.6 %collective-permute-start.8 = (bf16[3,128,128]{2,1,0:T(8,128)(2,1)S(1)}, bf16[3,128,128]{2,1,0:T(8,128)(2,1)S(1)}, u32[]{:S(2)}, u32[]{:S(2)}) collective-permute-start(bf16[3,128,128]{2,1,0:T(8,128)(2,1)S(1)} %broadcast_select_fusion), channel_id=1, source_target_pairs={{0,2},{1,3},{2,0},{3,1},{4,6},{5,7},{6,4},{7,5},{8,10},{9,11},{10,... | collective-permute-start | bytes 294920 | tf_op jit(solution)/shard_map/ppermute | solution.py:27
  14.0 0.7 %collective-permute-start = (bf16[1,2,256,128]{3,2,1,0:T(8,128)(2,1)S(1)}, bf16[1,2,256,128]{3,2,1,0:T(8,128)(2,1)S(1)}, u32[]{:S(2)}, u32[]{:S(2)}) collective-permute-start(bf16[1,2,256,128]{3,2,1,0:T(8,128)(2,1)S(1)} %get-tuple-element.12), channel_id=1, source_target_pairs={{0,12},{4,8},{8,4},{12,0},{16,28},{20,24},{24,20},{28,16},{1,13},{... | collective-permute-start | bytes 393224 | tf_op jit(solution)/shard_map/ppermute | solution.py:27
  14.7 4.7 %collective-permute-done.5.refs_2_ = bf16[1,2,256,128]{3,2,1,0:T(8,128)(2,1)S(1)} collective-permute-done((bf16[1,2,256,128]{3,2,1,0:T(8,128)(2,1)S(1)}, bf16[1,2,256,128]{3,2,1,0:T(8,128)(2,1)S(1)}, u32[]{:S(2)}, u32[]{:S(2)}) %collective-permute-start.5) | collective-permute-done | bytes 131104 | tf_op jit(solution)/shard_map/ppermute | solution.py:27
  19.4 1.6 %collective-permute-start.2 = (bf16[1,2,256,128]{3,2,1,0:T(8,128)(2,1)S(1)}, bf16[1,2,256,128]{3,2,1,0:T(8,128)(2,1)S(1)}, u32[]{:S(2)}, u32[]{:S(2)}) collective-permute-start(bf16[1,2,256,128]{3,2,1,0:T(8,128)(2,1)S(1)} %get-tuple-element.15), channel_id=1, source_target_pairs={{0,8},{4,12},{8,0},{12,4},{16,24},{20,28},{24,16},{28,20},{1,9},{5... | collective-permute-start | bytes 393224 | tf_op jit(solution)/shard_map/ppermute | solution.py:27
  21.0 0.8 %shard_map.98.refs_2_ = f32[3,128,128]{2,1,0:T(8,128)S(1)} custom-call(bf16[2,2,256,128]{3,2,1,0:T(8,128)(2,1)S(1)} %get-tuple-element.13.refs_0_, bf16[2,2,256,128]{3,2,1,0:T(8,128)(2,1)S(1)} %collective-permute-done.1.refs_1_, bf16[1,2,256,128]{3,2,1,0:T(8,128)(2,1)S(1)} %collective-permute-done.5.refs_2_, ...), custom_call_target="tpu_custom_call" | custom-call | tf_op jit(solution)/shard_map/pallas_call | solution.py:32
  21.8 0.4 %shard_map.99 = bf16[3,128,128]{2,1,0:T(8,128)(2,1)S(1)} custom-call(bf16[1,2,256,128]{3,2,1,0:T(8,128)(2,1)S(1)} %collective-permute-done.3.refs_0_, bf16[3,128,128]{2,1,0:T(8,128)(2,1)S(1)} %collective-permute-done.4.refs_3_.refs_1_, f32[3,128,128]{2,1,0:T(8,128)S(1)} %shard_map.98.refs_2_), custom_call_target="tpu_custom_call" | custom-call | tf_op jit(solution)/shard_map/pallas_call | solution.py:32
  22.2 0.4 %collective-permute-start.6 = (bf16[3,128,128]{2,1,0:T(8,128)(2,1)S(1)}, bf16[3,128,128]{2,1,0:T(8,128)(2,1)S(1)}, u32[]{:S(2)}, u32[]{:S(2)}) collective-permute-start(bf16[3,128,128]{2,1,0:T(8,128)(2,1)S(1)} %shard_map.99), channel_id=1, source_target_pairs={{0,16},{4,20},{8,24},{12,28},{16,0},{20,4},{24,8},{28,12},{1,17},{... | collective-permute-start | bytes 294920 | tf_op jit(solution)/shard_map/ppermute | solution.py:27
  22.7 1.8 %collective-permute-done.2.refs_2_ = bf16[1,2,256,128]{3,2,1,0:T(8,128)(2,1)S(1)} collective-permute-done((bf16[1,2,256,128]{3,2,1,0:T(8,128)(2,1)S(1)}, bf16[1,2,256,128]{3,2,1,0:T(8,128)(2,1)S(1)}, u32[]{:S(2)}, u32[]{:S(2)}) %collective-permute-start.2) | collective-permute-done | bytes 131104 | tf_op jit(solution)/shard_map/ppermute | solution.py:27
  24.5 0.8 %shard_map.95.refs_2_ = f32[3,128,128]{2,1,0:T(8,128)S(1)} custom-call(bf16[2,2,256,128]{3,2,1,0:T(8,128)(2,1)S(1)} %get-tuple-element.13.refs_0_, bf16[2,2,256,128]{3,2,1,0:T(8,128)(2,1)S(1)} %collective-permute-done.1.refs_1_, bf16[1,2,256,128]{3,2,1,0:T(8,128)(2,1)S(1)} %collective-permute-done.2.refs_2_, bf16[3,128,128]{2,1,0:T(8,128)(2,1)S(1)} %bitcast.13), custom_call_target="tpu_custom_call" | custom-call | tf_op jit(solution)/shard_map/pallas_call | solution.py:32
  25.4 0.4 %shard_map.96.refs_0_ = f32[3,128,128]{2,1,0:T(8,128)S(1)} custom-call(bf16[1,2,256,128]{3,2,1,0:T(8,128)(2,1)S(1)} %collective-permute-done.refs_0_, bf16[3,128,128]{2,1,0:T(8,128)(2,1)S(1)} %bitcast.14, f32[3,128,128]{2,1,0:T(8,128)S(1)} %shard_map.95.refs_2_), custom_call_target="tpu_custom_call" | custom-call | tf_op jit(solution)/shard_map/pallas_call | solution.py:32
  25.8 3.0 %collective-permute-done.6.refs_1_ = bf16[3,128,128]{2,1,0:T(8,128)(2,1)S(1)} collective-permute-done((bf16[3,128,128]{2,1,0:T(8,128)(2,1)S(1)}, bf16[3,128,128]{2,1,0:T(8,128)(2,1)S(1)}, u32[]{:S(2)}, u32[]{:S(2)}) %collective-permute-start.6) | collective-permute-done | bytes 98336 | tf_op jit(solution)/shard_map/ppermute | solution.py:27
  28.8 0.9 %shard_map.100 = (bf16[3,128,128]{2,1,0:T(8,128)(2,1)}, f32[3,128,128]{2,1,0:T(8,128)}, f32[3,128,128]{2,1,0:T(8,128)}) custom-call(f32[3,128,128]{2,1,0:T(8,128)S(1)} %shard_map.96.refs_0_, bf16[3,128,128]{2,1,0:T(8,128)(2,1)S(1)} %collective-permute-done.6.refs_1_, bf16[3,128,128]{2,1,0:T(8,128)(2,1)S(1)} %bitcast.15, ...), custom_call_target="tpu_custom_call" | custom-call | tf_op jit(solution)/shard_map/pallas_call | solution.py:32
  (11 shorter events, 0.0 us)
Async XLA Ops:
  0.6 11.7 %collective-permute-start.7 = (bf16[3,128,128]{2,1,0:T(8,128)(2,1)}, bf16[3,128,128]{2,1,0:T(8,128)(2,1)S(1)}, u32[]{:S(2)}, u32[]{:S(2)}) collective-permute-start(bf16[3,128,128]{2,1,0:T(8,128)(2,1)} %bitcast.11), channel_id=1, source_target_pairs={{0,1},{1,0},{2,3},{3,2},{4,5},{5,4},{6,7},{7,6},{8,9},{9,8},{10,11... | collective-permute-start | bytes 294920 | tf_op jit(solution)/shard_map/ppermute | solution.py:27
  3.7 10.3 %collective-permute-start.4 = (bf16[3,128,128]{2,1,0:T(8,128)(2,1)}, bf16[3,128,128]{2,1,0:T(8,128)(2,1)S(1)}, u32[]{:S(2)}, u32[]{:S(2)}) collective-permute-start(bf16[3,128,128]{2,1,0:T(8,128)(2,1)} %bitcast.12), channel_id=1, source_target_pairs={{0,16},{4,20},{8,24},{12,28},{16,0},{20,4},{24,8},{28,12},{1,17},{... | collective-permute-start | bytes 294920 | tf_op jit(solution)/shard_map/ppermute | solution.py:27
  8.2 4.0 %copy-start.3 = (s32[4]{0:T(128)S(1)}, s32[4]{0:T(128)}, u32[]{:S(2)}) copy-start(s32[4]{0:T(128)} %param.10) | copy-start | bytes 52
  8.3 4.0 %copy-start = (bf16[1,1,3,128,128]{4,3,2,1,0:T(8,128)(2,1)S(1)}, bf16[1,1,3,128,128]{4,3,2,1,0:T(8,128)(2,1)}, u32[]{:S(2)}) copy-start(bf16[1,1,3,128,128]{4,3,2,1,0:T(8,128)(2,1)} %param.11) | copy-start | bytes 294916
  8.3 12.7 %collective-permute-start.1 = (bf16[2,2,256,128]{3,2,1,0:T(8,128)(2,1)S(1)}, bf16[2,2,256,128]{3,2,1,0:T(8,128)(2,1)S(1)}, u32[]{:S(2)}, u32[]{:S(2)}) collective-permute-start(bf16[2,2,256,128]{3,2,1,0:T(8,128)(2,1)S(1)} %get-tuple-element.14), channel_id=1, source_target_pairs={{0,4},{4,0},{8,12},{12,8},{16,20},{20,16},{24,28},{28,24},{1,5},{5... | collective-permute-start | bytes 786440 | tf_op jit(solution)/shard_map/ppermute | solution.py:27
  10.0 18.7 %copy-start.1 = (f32[1,1,3,128,128]{4,3,2,1,0:T(8,128)S(1)}, f32[1,1,3,128,128]{4,3,2,1,0:T(8,128)}, u32[]{:S(2)}) copy-start(f32[1,1,3,128,128]{4,3,2,1,0:T(8,128)} %param.12) | copy-start | bytes 589828
  10.0 18.7 %copy-start.2 = (f32[1,1,3,128,128]{4,3,2,1,0:T(8,128)S(1)}, f32[1,1,3,128,128]{4,3,2,1,0:T(8,128)}, u32[]{:S(2)}) copy-start(f32[1,1,3,128,128]{4,3,2,1,0:T(8,128)} %param.13) | copy-start | bytes 589828
  10.1 11.8 %collective-permute-start.3 = (bf16[1,2,256,128]{3,2,1,0:T(8,128)(2,1)S(1)}, bf16[1,2,256,128]{3,2,1,0:T(8,128)(2,1)S(1)}, u32[]{:S(2)}, u32[]{:S(2)}) collective-permute-start(bf16[1,2,256,128]{3,2,1,0:T(8,128)(2,1)S(1)} %get-tuple-element.16), channel_id=1, source_target_pairs={{0,12},{4,8},{8,4},{12,0},{16,28},{20,24},{24,20},{28,16},{1,13},{... | collective-permute-start | bytes 393224 | tf_op jit(solution)/shard_map/ppermute | solution.py:27
  11.8 7.6 %collective-permute-start.5 = (bf16[1,2,256,128]{3,2,1,0:T(8,128)(2,1)S(1)}, bf16[1,2,256,128]{3,2,1,0:T(8,128)(2,1)S(1)}, u32[]{:S(2)}, u32[]{:S(2)}) collective-permute-start(bf16[1,2,256,128]{3,2,1,0:T(8,128)(2,1)S(1)} %get-tuple-element.17), channel_id=1, source_target_pairs={{0,8},{4,12},{8,0},{12,4},{16,24},{20,28},{24,16},{28,20},{1,9},{5... | collective-permute-start | bytes 393224 | tf_op jit(solution)/shard_map/ppermute | solution.py:27
  12.3 10.3 %collective-permute-start.8 = (bf16[3,128,128]{2,1,0:T(8,128)(2,1)S(1)}, bf16[3,128,128]{2,1,0:T(8,128)(2,1)S(1)}, u32[]{:S(2)}, u32[]{:S(2)}) collective-permute-start(bf16[3,128,128]{2,1,0:T(8,128)(2,1)S(1)} %broadcast_select_fusion), channel_id=1, source_target_pairs={{0,2},{1,3},{2,0},{3,1},{4,6},{5,7},{6,4},{7,5},{8,10},{9,11},{10,... | collective-permute-start | bytes 294920 | tf_op jit(solution)/shard_map/ppermute | solution.py:27
  14.0 11.4 %collective-permute-start = (bf16[1,2,256,128]{3,2,1,0:T(8,128)(2,1)S(1)}, bf16[1,2,256,128]{3,2,1,0:T(8,128)(2,1)S(1)}, u32[]{:S(2)}, u32[]{:S(2)}) collective-permute-start(bf16[1,2,256,128]{3,2,1,0:T(8,128)(2,1)S(1)} %get-tuple-element.12), channel_id=1, source_target_pairs={{0,12},{4,8},{8,4},{12,0},{16,28},{20,24},{24,20},{28,16},{1,13},{... | collective-permute-start | bytes 393224 | tf_op jit(solution)/shard_map/ppermute | solution.py:27
  19.4 5.1 %collective-permute-start.2 = (bf16[1,2,256,128]{3,2,1,0:T(8,128)(2,1)S(1)}, bf16[1,2,256,128]{3,2,1,0:T(8,128)(2,1)S(1)}, u32[]{:S(2)}, u32[]{:S(2)}) collective-permute-start(bf16[1,2,256,128]{3,2,1,0:T(8,128)(2,1)S(1)} %get-tuple-element.15), channel_id=1, source_target_pairs={{0,8},{4,12},{8,0},{12,4},{16,24},{20,28},{24,16},{28,20},{1,9},{5... | collective-permute-start | bytes 393224 | tf_op jit(solution)/shard_map/ppermute | solution.py:27
  22.2 6.5 %collective-permute-start.6 = (bf16[3,128,128]{2,1,0:T(8,128)(2,1)S(1)}, bf16[3,128,128]{2,1,0:T(8,128)(2,1)S(1)}, u32[]{:S(2)}, u32[]{:S(2)}) collective-permute-start(bf16[3,128,128]{2,1,0:T(8,128)(2,1)S(1)} %shard_map.99), channel_id=1, source_target_pairs={{0,16},{4,20},{8,24},{12,28},{16,0},{20,4},{24,8},{28,12},{1,17},{... | collective-permute-start | bytes 294920 | tf_op jit(solution)/shard_map/ppermute | solution.py:27
